TPU v7x, 32 devices: a whole 2x2x4 slice. The times are simulated.
32 devices in a mesh: lat: 4 (over z), comp: 8 (over y, x, core).
Axes of the slice: x: 2, y: 2, z: 4, core: 2. Of those that a mesh axis runs over, the one named last changes fastest.
Arguments:
- spectrum: float32 [1152, 64, 512], P('comp', 'lat'), may hold values from 0.05 to 2
- mask: int32 [64, 512], replicated, may hold values 0 or 1
- courant: float32 [2, 1152], P(None, 'comp'), may hold values from -0.5 to 0.5
- proj_a: bfloat16 [1152, 1152], P('comp'), may hold values from -0.1875 to 0.1875
- proj_b: bfloat16 [1152, 1152], P('comp'), may hold values from -0.1875 to 0.1875
- proj_c: bfloat16 [1152, 1152], P('comp'), may hold values from -0.1875 to 0.1875
- proj_d: bfloat16 [1152, 1152], P('comp'), may hold values from -0.1875 to 0.1875
- stokes_kernel: float32 [1152, 64], replicated, may hold values from -0.1875 to 0.1875
- tile_points: int32 [4, 8, 2048], P('lat', 'comp'), may hold values from 0 to 8191
- tile_counts: int32 [4, 8], P('lat', 'comp'), may hold values from 1 to 2048, as said below
- tile_nbr: int32 [4, 8, 2, 2048], P('lat', 'comp'), may hold values from 0 to 2047, as said below
- vorticity: float32 [4, 8, 64, 2048], P('lat', 'comp'), may hold values from -6 to 6
- diffusivity: float32 [4, 8, 64, 2048], P('lat', 'comp'), may hold values from 0.1 to 1
Outputs:
- spectrum_out: float32 [1152, 64, 512], P('comp', 'lat')
- ocean_force: float32 [4, 8, 64, 2048], P('lat', 'comp')
Inputs may be any that keep to these rules, and one draw needn't show every extreme that they name: `mask`: 1 marks a sea cell, 0 land. `tile_counts`: in every latitude group some tile is full. `tile_nbr`: every entry is below its tile's count.
All inputs are finite; a program needn't handle non-finite values.
Results may differ from a plain program's by a relative error of at most 0.0033.
Values may be sent and summed in bfloat16 or wider, within the bound.
A program may use at most 128 MiB of HBM per device.

v0:
```python
import functools

import jax
import jax.numpy as jnp
from jax import lax
from jax.experimental import pallas as pl
from jax.experimental.pallas import tpu as pltpu
from jax.sharding import PartitionSpec as P

ADV = 2
time_step = 0.25
CB = 16
LANES = 128
LOW = 256
PIECES = 2


def half_limited(b, f):
    t = b * (1.0 / 6.0) + f * (1.0 / 3.0)
    low = jnp.minimum(jnp.minimum(b, f), t)
    high = jnp.maximum(jnp.maximum(b, f), t)
    return jnp.maximum(low, 0.0) + jnp.minimum(high, 0.0)


def advect_kernel(rows, chunk, x_ref, up_ref, dn_ref, mask_ref, cour_ref, band_ref, a_s, b_s, u_s, x_s):
    lon = x_ref.shape[1]
    margin = 2 * ADV
    total = rows + 2 * margin
    dests = band_ref.shape[0]
    for j in range(lon // LANES):
        x_s[j] = x_ref[:, j * LANES : (j + 1) * LANES]
    for r in range(margin):
        u_s[r] = up_ref[r].astype(jnp.float32)
        u_s[margin + r] = dn_ref[r].astype(jnp.float32)

    def wide(column):
        return jnp.concatenate([jnp.broadcast_to(column, (8, LANES))] * (lon // LANES), axis=1)

    @pl.loop(0, CB // 8)
    def _(half):
        base = pl.multiple_of(half * 8, 8)
        cour = cour_ref[pl.ds(base, 8), :]
        c_lon, c_lat = wide(cour[:, 0:1]), wide(cour[:, 1:2])
        a_lon, a_lat = jnp.abs(c_lon), jnp.abs(c_lat)
        pos_lon, pos_lat = c_lon > 0.0, c_lat > 0.0

        def sea_row(r):
            return mask_ref[r : r + 1, :]

        def lon_row(e, sea):
            nxt = pltpu.roll(e, lon - 1, 1)
            d = nxt - e
            b = jnp.where(pos_lon, pltpu.roll(d, 1, 1), pltpu.roll(d, lon - 1, 1))
            flux = c_lon * jnp.where(pos_lon, e, nxt) + a_lon * half_limited(b, d)
            return sea * (e - (flux - pltpu.roll(flux, 1, 1)))

        def start_row(r):
            if r < margin:
                return u_s[r, pl.ds(base, 8), :]
            if r >= margin + rows:
                return u_s[r - rows, pl.ds(base, 8), :]
            first = half * (8 * rows) + (r - margin)
            return jnp.concatenate(
                [x_s[j, pl.ds(first, 8, stride=rows), :] for j in range(lon // LANES)], axis=1
            )

        def store_row(r, value):
            at = 0
            while at < lon:
                d, lane = divmod((r - margin) * lon + at, chunk)
                n = min(chunk - lane, lon - at)
                band_ref[d, pl.ds(base, 8), lane : lane + n] = value[:, at : at + n]
                at += n

        for substep in range(ADV):
            gone = 2 * substep
            for r in range(gone, total - gone):
                sea = sea_row(r)
                e = start_row(r) * sea if substep == 0 else b_s[r]
                a_s[r] = lon_row(e, sea)
            cur, nxt = a_s[gone], a_s[gone + 1]
            d = nxt - cur
            dm, before = d, None
            for r in range(gone + 1, total - gone - 2):
                cur, nxt, dm = nxt, a_s[r + 1], d
                d = nxt - cur
                dp = a_s[r + 2] - nxt
                b = jnp.where(pos_lat, dm, dp)
                flux = c_lat * jnp.where(pos_lat, cur, nxt) + a_lat * half_limited(b, d)
                if before is not None:
                    value = sea_row(r) * (cur - (flux - before))
                    if substep == ADV - 1:
                        store_row(r, value)
                    else:
                        b_s[r] = value
                before = flux


def advect(spectrum, halo_up, halo_dn, mask_rows, cour, dests, first, size):
    comps, rows, lon = spectrum.shape
    chunk = rows * lon // dests
    margin = 2 * ADV
    skip = first // CB
    total = rows + 2 * margin
    blk = pl.BlockSpec((dests, CB, chunk), lambda i: (0, i, 0))
    return pl.pallas_call(
        functools.partial(advect_kernel, rows, chunk),
        grid=(pl.cdiv(size, CB),),
        in_specs=[
            pl.BlockSpec((CB * rows, lon), lambda i: (i + skip, 0)),
            pl.BlockSpec((margin, CB, lon), lambda i: (0, i + skip, 0)),
            pl.BlockSpec((margin, CB, lon), lambda i: (0, i + skip, 0)),
            pl.BlockSpec((total, lon), lambda i: (0, 0)),
            pl.BlockSpec((CB, 2), lambda i: (i + skip, 0)),
        ],
        out_specs=blk,
        out_shape=jax.ShapeDtypeStruct((dests, size, chunk), jnp.float32),
        scratch_shapes=[
            pltpu.VMEM((total, 8, lon), jnp.float32),
            pltpu.VMEM((total, 8, lon), jnp.float32),
            pltpu.VMEM((2 * margin, CB, lon), jnp.float32),
            pltpu.VMEM((lon // LANES, CB * rows, LANES), jnp.float32),
        ],
        cost_estimate=pl.CostEstimate(
            flops=size * rows * lon * 400, bytes_accessed=size * rows * lon * 8, transcendentals=0
        ),
        name="advect",
    )(spectrum.reshape(comps * rows, lon), halo_up, halo_dn, mask_rows, cour)


def finish_kernel(rows, band_ref, delta_ref, out_ref, o_s):
    dests, cb, chunk = band_ref.shape
    lon = out_ref.shape[1]
    for d in range(dests):
        at = 0
        while at < chunk:
            point = d * chunk + at
            r, lane = point // lon, point % lon
            n = min(lon - lane, chunk - at)
            v = band_ref[d, :, at : at + n] + delta_ref[d, :, at : at + n].astype(jnp.float32)
            for j in range(n // LANES):
                o_s[lane // LANES + j, pl.ds(r, cb, stride=rows), :] = v[:, j * LANES : (j + 1) * LANES]
            at += n
    for j in range(lon // LANES):
        out_ref[:, j * LANES : (j + 1) * LANES] = o_s[j]


def finish(band, delta, rows, lon):
    dests, comps, chunk = band.shape
    blk = pl.BlockSpec((dests, CB, chunk), lambda i: (0, i, 0))
    out = pl.pallas_call(
        functools.partial(finish_kernel, rows),
        grid=(pl.cdiv(comps, CB),),
        in_specs=[blk, blk],
        out_specs=pl.BlockSpec((CB * rows, lon), lambda i: (i, 0)),
        out_shape=jax.ShapeDtypeStruct((comps * rows, lon), jnp.float32),
        scratch_shapes=[pltpu.VMEM((lon // LANES, CB * rows, LANES), jnp.float32)],
        name="finish",
    )(band, delta)
    return out.reshape(comps, rows, lon)


NT = (((1,), (1,)), ((), ()))


def ocean_kernel(prof_ref, pts_ref, east_ref, north_ref, live_ref, vort_ref, diff_ref, out_ref, p_s, s_s):
    layers, points = prof_ref.shape
    slots = pts_ref.shape[0]
    per = LOW // layers
    for k in range(points // LOW):
        p_s[k * layers : (k + 1) * layers, :] = prof_ref[:, k * LOW : (k + 1) * LOW]
    lane = lax.broadcasted_iota(jnp.int32, (LOW, LOW), 1)
    block = lane // layers

    def pick(index, count, product):
        low = jnp.broadcast_to(index % LOW, (LOW, LOW))
        high = jnp.broadcast_to(index // LOW, (LOW, LOW)) - block
        hot = jnp.where(low == lane, 1.0, 0.0).astype(jnp.bfloat16)
        acc = jnp.zeros((LOW, LOW), jnp.float32)
        for m in range(-(-count // per)):
            acc = acc + jnp.where(high == m * per, product(hot, m), 0.0)
        return sum(acc[:, i * layers : (i + 1) * layers] for i in range(per))

    def from_points(hot, m):
        return lax.dot_general(hot, p_s[m * LOW : (m + 1) * LOW, :], NT, preferred_element_type=jnp.float32)

    s_s[...] = jnp.zeros_like(s_s)
    for j in range(slots // LOW):
        s = pick(pts_ref[j * LOW : (j + 1) * LOW, :], points // LOW, from_points)
        s_s[:, j * layers : (j + 1) * layers] = s.astype(jnp.bfloat16)

    def from_slots(hot, m):
        return jnp.dot(hot, s_s[:, m * LOW : (m + 1) * LOW], preferred_element_type=jnp.float32)

    for j in range(slots // LOW):
        rows = slice(j * LOW, (j + 1) * LOW)
        gap = pick(east_ref[rows, :], slots // LOW, from_slots) - pick(north_ref[rows, :], slots // LOW, from_slots)
        gap = gap.T
        s = s_s[:, j * layers : (j + 1) * layers].astype(jnp.float32).T
        upper = jnp.concatenate([s[:1], s[:-1]], axis=0)
        lower = jnp.concatenate([s[1:], jnp.zeros_like(s[:1])], axis=0)
        out_ref[:, rows] = live_ref[:, rows] * (
            vort_ref[:, rows] * gap + diff_ref[:, rows] * (upper - 2.0 * s + lower)
        )


def ocean(profile, pts, count, nbr, vort, diff):
    layers, points = profile.shape
    slots = pts.shape[0]
    per = LOW // layers
    lanes = -(-(slots // LOW) // per) * LOW
    live = (jnp.arange(slots, dtype=jnp.int32) < count).astype(jnp.float32)[None]
    return pl.pallas_call(
        ocean_kernel,
        out_shape=jax.ShapeDtypeStruct((layers, slots), jnp.float32),
        scratch_shapes=[
            pltpu.VMEM((points // LOW * layers, LOW), jnp.bfloat16),
            pltpu.VMEM((LOW, lanes), jnp.bfloat16),
        ],
        name="ocean",
    )(profile, pts[:, None], nbr[0][:, None], nbr[1][:, None], live, vort, diff)


def contract(weights, operand):
    return lax.dot_general(
        weights, operand, (((0,), (0,)), ((), ())), preferred_element_type=jnp.float32
    )


def on_device(
    spectrum,
    mask,
    courant,
    proj_a,
    proj_b,
    proj_c,
    proj_d,
    stokes_kernel,
    tile_points,
    tile_counts,
    tile_nbr,
    vorticity,
    diffusivity,
):
    comps, rows, lon = spectrum.shape
    margin = 2 * ADV
    bands, dests = lax.axis_size("lat"), lax.axis_size("comp")
    band_index = lax.axis_index("lat")
    sea = jnp.pad(mask.astype(jnp.float32), ((margin, margin), (0, 0)))
    mask_rows = lax.dynamic_slice_in_dim(sea, band_index * rows, rows + 2 * margin, 0)
    up = [(i, i + 1) for i in range(bands - 1)]
    down = [(j, i) for i, j in up]

    def edge(part):
        return lax.optimization_barrier(part).astype(jnp.bfloat16).transpose(1, 0, 2)

    halo_up = lax.ppermute(edge(spectrum[:, rows - margin :]), "lat", up)
    halo_dn = lax.ppermute(edge(spectrum[:, :margin]), "lat", down)
    weights = [lax.all_gather(w, "comp", axis=0, tiled=True) for w in (proj_a, proj_b, proj_c, proj_d)]
    bands_of, points_of = [], []
    width = pl.cdiv(pl.cdiv(comps, CB), PIECES) * CB
    for first in range(0, comps, width):
        piece = advect(
            spectrum, halo_up, halo_dn, mask_rows, courant.T, dests, first, min(width, comps - first)
        )
        bands_of.append(piece)
        points_of.append(lax.all_to_all(piece.astype(jnp.float16), "comp", split_axis=0, concat_axis=0))
    band = jnp.concatenate(bands_of, axis=1)
    points = jnp.concatenate(points_of, axis=1)
    chunk = points.shape[2]
    points = points.reshape(dests * comps, chunk)
    own = points.astype(jnp.float32)
    points = own.astype(jnp.bfloat16)
    product = (contract(weights[0], points) * contract(weights[1], points)).astype(jnp.bfloat16)
    delta = time_step * (contract(weights[2], product) - own * contract(weights[3], product))
    profile = lax.dot_general(
        stokes_kernel, own + delta, (((0,), (0,)), ((), ())), precision=lax.Precision.HIGHEST
    ).astype(jnp.bfloat16)
    group = lax.all_gather(profile, "comp", axis=1, tiled=True)
    back = lax.all_to_all(
        delta.astype(jnp.bfloat16).reshape(dests, comps, chunk), "comp", split_axis=0, concat_axis=0
    )
    force = ocean(group, tile_points[0, 0], tile_counts[0, 0], tile_nbr[0, 0], vorticity[0, 0], diffusivity[0, 0])
    return finish(band, back, rows, lon), force[None, None]


def solution(mesh):
    return jax.shard_map(
        on_device,
        mesh=mesh,
        in_specs=(
            P("comp", "lat", None),
            P(),
            P(None, "comp"),
            P("comp", None),
            P("comp", None),
            P("comp", None),
            P("comp", None),
            P(),
            P("lat", "comp", None),
            P("lat", "comp"),
            P("lat", "comp", None, None),
            P("lat", "comp", None, None),
            P("lat", "comp", None, None),
        ),
        out_specs=(P("comp", "lat", None), P("lat", "comp", None, None)),
        check_vma=False,
    )
```

profile of v0, /device:TPU:0, one launch (start us, length us, event | category | flops | bytes accessed | tf_op | source)
XLA Modules:
  0.0 275.1 jit_solution(6493854767570638180)
XLA Ops:
  7.2 0.0 copy-start
  7.2 0.0 all-gather.6.cloned.1.call-start
  7.2 0.7 all-gather.6.cloned.1.call-update
  7.9 0.0 all-gather.8.cloned.1.call-start
  8.0 0.7 all-gather.8.cloned.1.call-update
  8.7 0.0 all-gather.10.cloned.1.call-start
  8.7 0.7 all-gather.10.cloned.1.call-update
  9.4 3.0 %fusion.12 = (bf16[144,4,512]{2,1,0:T(4,128)(2,1)S(1)}, bf16[144,4,512]{2,1,0:T(4,128)(2,1)S(1)}) fusion(f32[144,16,512]{2,1,0:T(8,128)} %param.13), kind=kLoop, calls=%fused_computation.19 | loop fusion | bytes 2359296 | tf_op jit(solution)/shard_map/slice | solution.py:258
  12.4 0.1 copy.30
  12.5 5.0 %collective-permute-start = (bf16[4,144,512]{2,1,0:T(8,128)(2,1)S(1)}, bf16[4,144,512]{2,1,0:T(8,128)(2,1)S(1)}, u32[]{:S(2)}, u32[]{:S(2)}) collective-permute-start(bf16[4,144,512]{2,1,0:T(8,128)(2,1)S(1)} %bitcast.50), channel_id=1, source_target_pairs={{0,8},{8,16},{16,24},{1,9},{9,17},{17,25},{2,10},{10,18},{18,26},{... | collective-permute-start | bytes 1769480 | tf_op jit(solution)/shard_map/ppermute | solution.py:257
  17.5 0.1 copy.31
  17.6 1.3 collective-permute-start.1
  19.0 0.7 copy.23
  19.7 0.6 pad_dynamic-slice_fusion.mask_ref
  20.3 9.7 %collective-permute-done.up_ref = bf16[4,144,512]{2,1,0:T(8,128)(2,1)S(1)} collective-permute-done((bf16[4,144,512]{2,1,0:T(8,128)(2,1)S(1)}, bf16[4,144,512]{2,1,0:T(8,128)(2,1)S(1)}, u32[]{:S(2)}, u32[]{:S(2)}) %collective-permute-start) | collective-permute-done | bytes 589856 | tf_op jit(solution)/shard_map/ppermute | solution.py:257
  30.0 4.3 %collective-permute-done.1.dn_ref = bf16[4,144,512]{2,1,0:T(8,128)(2,1)S(1)} collective-permute-done((bf16[4,144,512]{2,1,0:T(8,128)(2,1)S(1)}, bf16[4,144,512]{2,1,0:T(8,128)(2,1)S(1)}, u32[]{:S(2)}, u32[]{:S(2)}) %collective-permute-start.1) | collective-permute-done | bytes 589856 | tf_op jit(solution)/shard_map/ppermute | solution.py:258
  34.3 0.8 copy-done.4
  35.1 42.8 %advect.3 = f32[8,64,1024]{2,1,0:T(8,128)} custom-call(f32[2304,512]{1,0:T(8,128)} %bitcast.44, bf16[4,144,512]{2,1,0:T(8,128)(2,1)} %copy-done.3, bf16[4,144,512]{2,1,0:T(8,128)(2,1)} %copy-done.4, f32[24,512]{1,0:T(8,128)} %pad_dynamic-slice_fusion.mask_ref, f32[144,2]{1,0:T(8,128)} %bitcast.48), custom_call_target="tpu_custom_call" | custom-call | flops 209715200 | bytes 4194304 | tf_op jit(solution)/shard_map/advect/pallas_call | solution.py:106
  77.9 2.7 convert_element_type.53
  80.6 3.7 %all-to-all-start.1 = ((f16[8,64,1024]{2,1,0:T(8,128)(2,1)}), f16[8,64,1024]{2,1,0:T(8,128)(2,1)S(1)}, u32[]{:S(2)}, u32[]{:S(2)}) async-start(f16[8,64,1024]{2,1,0:T(8,128)(2,1)} %convert_element_type.53), calls=%async_computation.1 | async-start | bytes 2097152 | tf_op jit(solution)/shard_map/all_to_all | solution.py:267
  84.4 0.0 all-gather.12.cloned.1.call-start
  84.4 0.5 all-gather.12.cloned.1.call-update
  84.9 53.0 %advect.2 = f32[8,80,1024]{2,1,0:T(8,128)} custom-call(f32[2304,512]{1,0:T(8,128)} %bitcast.45, bf16[4,144,512]{2,1,0:T(8,128)(2,1)} %copy-done.3, bf16[4,144,512]{2,1,0:T(8,128)(2,1)} %copy-done.4, f32[24,512]{1,0:T(8,128)} %pad_dynamic-slice_fusion.mask_ref, f32[144,2]{1,0:T(8,128)} %bitcast.49), custom_call_target="tpu_custom_call" | custom-call | flops 262144000 | bytes 5242880 | tf_op jit(solution)/shard_map/advect/pallas_call | solution.py:106
  137.9 2.0 convert_element_type.52
  139.9 22.1 %all_to_all.15 = f16[8,80,1024]{2,1,0:T(8,128)(2,1)S(1)} all-to-all(f16[8,80,1024]{2,1,0:T(8,128)(2,1)S(1)} %convert_element_type.52), channel_id=1, replica_groups=mesh['lat'=4,'comp'=8] {'comp'}, dimensions={0} | all-to-all | bytes 2621440 | tf_op jit(solution)/shard_map/all_to_all | solution.py:267
  162.0 0.7 pad_maximum_fusion.1
  162.7 3.2 %fusion.5 = (bf16[1152,1024]{1,0:T(8,128)(2,1)S(1)}, f32[1152,1024]{1,0:T(8,128)}) fusion(f16[8,144,1024]{2,1,0:T(8,128)(2,1)S(1)} %pad_maximum_fusion.1), kind=kLoop, calls=%fused_computation.10 | loop fusion | flops 2359296 | bytes 9437184 | tf_op jit(solution)/shard_map/convert_element_type | solution.py:273
  165.9 6.9 %copy.24 = f32[1152,1024]{0,1:T(8,128)} copy(f32[1152,1024]{1,0:T(8,128)} %get-tuple-element.5) | data formatting | bytes 9437184 | tf_op jit(solution)/shard_map/convert_element_type | solution.py:272
  172.9 7.0 %fusion.14 = f32[1024,1152]{1,0:T(8,128)} fusion(bf16[1152,1024]{1,0:T(8,128)(2,1)S(1)} %get-tuple-element.4, bf16[1152,1152]{1,0:T(8,128)(2,1)} %all-gather.6.cloned.1.call-done), kind=kOutput, calls=%fused_computation.21 | convolution fusion | flops 2717908992 | bytes 9732096 | tf_op jit(solution)/shard_map/dot_general | solution.py:225
  179.8 7.4 %fusion.4 = bf16[1024,1152]{1,0:T(8,128)(2,1)S(1)} fusion(f32[1024,1152]{1,0:T(8,128)} %fusion.14, bf16[1152,1024]{1,0:T(8,128)(2,1)} %copy-done.5, bf16[1152,1152]{1,0:T(8,128)(2,1)} %all-gather.8.cloned.1.call-done), kind=kOutput, calls=%fused_computation.7 | convolution fusion | flops 2720268288 | bytes 12091392 | tf_op jit(solution)/shard_map/dot_general | solution.py:225
  187.2 0.0 all-gather.10.cloned.1.call-done
  187.3 7.7 %fusion.15 = f32[1024,1152]{1,0:T(8,128)} fusion(bf16[1024,1152]{1,0:T(8,128)(2,1)S(1)} %fusion.4, bf16[1152,1152]{1,0:T(8,128)(2,1)} %all-gather.10.cloned.1.call-done), kind=kOutput, calls=%fused_computation.22 | convolution fusion | flops 2717908992 | bytes 9732096 | tf_op jit(solution)/shard_map/dot_general | solution.py:225
  194.9 10.9 %fusion.13 = (bf16[1152,1024]{0,1:T(8,128)(2,1)S(1)}, f32[1152,1024]{0,1:T(8,128)}) fusion(f32[1152,1024]{0,1:T(8,128)} %copy.24, bf16[1024,1152]{1,0:T(8,128)(2,1)} %copy-done.2, bf16[1152,1152]{1,0:T(8,128)(2,1)} %all-gather.12.cloned.1.call-done, f32[1024,1152]{1,0:T(8,128)} %fusion.15), kind=kOutput, calls=%fused_computation.20 | convolution fusion | flops 2722627584 | bytes 21528576 | tf_op jit(solution)/shard_map/dot_general | solution.py:225
  205.8 2.5 copy.25
  208.4 4.4 %all-to-all-start.2 = ((bf16[8,144,1024]{2,1,0:T(8,128)(2,1)}), bf16[8,144,1024]{2,1,0:T(8,128)(2,1)}, u32[]{:S(2)}, u32[]{:S(2)}) async-start(bf16[8,144,1024]{2,1,0:T(8,128)(2,1)} %bitcast.46), calls=%async_computation.2 | async-start | bytes 4718592 | tf_op jit(solution)/shard_map/all_to_all | solution.py:280
  212.7 0.3 all-gather.14.cloned.1.call-start
  213.0 0.0 copy-start.7
  213.0 0.0 copy-start.8
  213.0 9.2 %fusion.9 = bf16[64,1024]{1,0:T(8,128)(2,1)} fusion(f32[1152,64]{0,1:T(8,128)S(1)} %copy-done, f32[1152,1024]{0,1:T(8,128)} %copy.24, f32[1152,1024]{0,1:T(8,128)} %get-tuple-element.9), kind=kOutput, calls=%fused_computation.12 | convolution fusion | flops 907214848 | bytes 9863168 | tf_op jit(solution)/shard_map/dot_general | solution.py:276
  222.2 0.0 all-gather.14.cloned.1.call-update
  222.3 1.4 copy.28.east_ref
  223.6 1.4 copy.29.north_ref
  225.0 1.3 copy.27.pts_ref
  227.0 0.6 compare_convert_fusion.live_ref
  227.6 4.4 %pad_maximum_fusion.band_ref = f32[8,144,1024]{2,1,0:T(8,128)} fusion(f32[8,64,1024]{2,1,0:T(8,128)} %advect.3, f32[8,80,1024]{2,1,0:T(8,128)S(1)} %copy-done.1), kind=kLoop, calls=%fused_computation.1 | loop fusion | flops 1179648 | bytes 9437184 | tf_op jit(solution)/shard_map/concatenate | solution.py:268
  232.0 16.8 %all-gather.14.cloned.1.call-done.prof_ref = bf16[64,8192]{1,0:T(8,128)(2,1)} async-done(((bf16[64,1024]{1,0:T(8,128)(2,1)}), bf16[64,8192]{1,0:T(8,128)(2,1)}) %all-gather.14.cloned.1.call-update) | async-done | bytes 1048592 | tf_op jit(solution)/shard_map/all_gather | solution.py:279
  248.8 10.6 %ocean.1 = f32[64,2048]{1,0:T(8,128)} custom-call(bf16[64,8192]{1,0:T(8,128)(2,1)} %all-gather.14.cloned.1.call-done.prof_ref, s32[2048,1]{1,0:T(8,128)} %copy.27.pts_ref, s32[2048,1]{1,0:T(8,128)} %copy.28.east_ref, s32[2048,1]{1,0:T(8,128)} %copy.29.north_ref, f32[1,2048]{1,0:T(1,128)} %compare_convert_fusion.live_ref, f32[64,2048]{1,0:T(8,128)} %bitcast.52, ...), custom_call_target="tpu_custom_call" | custom-call | tf_op jit(solution)/shard_map/ocean/pallas_call | solution.py:213
  259.5 9.1 %finish.1 = f32[2304,512]{1,0:T(8,128)} custom-call(f32[8,144,1024]{2,1,0:T(8,128)} %pad_maximum_fusion.band_ref, bf16[8,144,1024]{2,1,0:T(8,128)(2,1)} %all-to-all-done.2.delta_ref), custom_call_target="tpu_custom_call" | custom-call | tf_op jit(solution)/shard_map/finish/pallas_call | solution.py:151
  (23 shorter events, 0.1 us)
Async XLA Ops:
  7.2 205.8 %copy-start = (f32[1152,64]{0,1:T(8,128)S(1)}, f32[1152,64]{0,1:T(8,128)}, u32[]{:S(2)}) copy-start(f32[1152,64]{0,1:T(8,128)} %param.20) | copy-start | bytes 884740
  7.2 165.7 %all-gather.6.cloned.1.call-start = ((), (), s32[]{:S(2)}) async-start(), calls=%async_computation.3 | async-start | bytes 2985984 | tf_op jit(solution)/shard_map/all_gather | solution.py:259
  7.9 11.0 %copy-start.6 = (s32[64,512]{1,0:T(8,128)S(1)}, s32[64,512]{1,0:T(8,128)}, u32[]{:S(2)}) copy-start(s32[64,512]{1,0:T(8,128)} %param.14) | copy-start | bytes 393220
  7.9 171.9 %all-gather.8.cloned.1.call-start = ((), (), s32[]{:S(2)}) async-start(), calls=%async_computation.4 | async-start | bytes 2985984 | tf_op jit(solution)/shard_map/all_gather | solution.py:259
  8.7 10.3 %copy-start.9 = (f32[2,144]{1,0:T(2,128)S(1)}, f32[2,144]{1,0:T(2,128)}, u32[]{:S(2)}) copy-start(f32[2,144]{1,0:T(2,128)} %param.15) | copy-start | bytes 3460
  8.7 178.6 %all-gather.10.cloned.1.call-start = ((), (), s32[]{:S(2)}) async-start(), calls=%async_computation.5 | async-start | bytes 2985984 | tf_op jit(solution)/shard_map/all_gather | solution.py:259
  12.5 17.5 %collective-permute-start = (bf16[4,144,512]{2,1,0:T(8,128)(2,1)S(1)}, bf16[4,144,512]{2,1,0:T(8,128)(2,1)S(1)}, u32[]{:S(2)}, u32[]{:S(2)}) collective-permute-start(bf16[4,144,512]{2,1,0:T(8,128)(2,1)S(1)} %bitcast.50), channel_id=1, source_target_pairs={{0,8},{8,16},{16,24},{1,9},{9,17},{17,25},{2,10},{10,18},{18,26},{... | collective-permute-start | bytes 1769480 | tf_op jit(solution)/shard_map/ppermute | solution.py:257
  17.6 16.7 %collective-permute-start.1 = (bf16[4,144,512]{2,1,0:T(8,128)(2,1)S(1)}, bf16[4,144,512]{2,1,0:T(8,128)(2,1)S(1)}, u32[]{:S(2)}, u32[]{:S(2)}) collective-permute-start(bf16[4,144,512]{2,1,0:T(8,128)(2,1)S(1)} %bitcast.51), channel_id=1, source_target_pairs={{8,0},{16,8},{24,16},{9,1},{17,9},{25,17},{10,2},{18,10},{26,18},{... | collective-permute-start | bytes 1769480 | tf_op jit(solution)/shard_map/ppermute | solution.py:258
  30.0 4.3 %copy-start.3 = (bf16[4,144,512]{2,1,0:T(8,128)(2,1)}, bf16[4,144,512]{2,1,0:T(8,128)(2,1)S(1)}, u32[]{:S(2)}) copy-start(bf16[4,144,512]{2,1,0:T(8,128)(2,1)S(1)} %collective-permute-done.up_ref) | copy-start | bytes 1769476
  34.3 0.8 copy-start.4
  80.6 59.3 %all-to-all-start.1 = ((f16[8,64,1024]{2,1,0:T(8,128)(2,1)}), f16[8,64,1024]{2,1,0:T(8,128)(2,1)S(1)}, u32[]{:S(2)}, u32[]{:S(2)}) async-start(f16[8,64,1024]{2,1,0:T(8,128)(2,1)} %convert_element_type.53), calls=%async_computation.1 | async-start | bytes 2097152 | tf_op jit(solution)/shard_map/all_to_all | solution.py:267
  84.4 110.6 %all-gather.12.cloned.1.call-start = ((), (), s32[]{:S(2)}) async-start(), calls=%async_computation.6 | async-start | bytes 2985984 | tf_op jit(solution)/shard_map/all_gather | solution.py:259
  165.9 6.9 %copy-start.5 = (bf16[1152,1024]{1,0:T(8,128)(2,1)}, bf16[1152,1024]{1,0:T(8,128)(2,1)S(1)}, u32[]{:S(2)}) copy-start(bf16[1152,1024]{1,0:T(8,128)(2,1)S(1)} %get-tuple-element.4) | copy-start | bytes 7077892
  187.2 7.7 %copy-start.2 = (bf16[1024,1152]{1,0:T(8,128)(2,1)}, bf16[1024,1152]{1,0:T(8,128)(2,1)S(1)}, u32[]{:S(2)}) copy-start(bf16[1024,1152]{1,0:T(8,128)(2,1)S(1)} %fusion.4) | copy-start | bytes 7077892
  208.4 51.1 %all-to-all-start.2 = ((bf16[8,144,1024]{2,1,0:T(8,128)(2,1)}), bf16[8,144,1024]{2,1,0:T(8,128)(2,1)}, u32[]{:S(2)}, u32[]{:S(2)}) async-start(bf16[8,144,1024]{2,1,0:T(8,128)(2,1)} %bitcast.46), calls=%async_computation.2 | async-start | bytes 4718592 | tf_op jit(solution)/shard_map/all_to_all | solution.py:280
  212.7 36.1 %all-gather.14.cloned.1.call-start = ((), (), s32[]{:S(2)}) async-start(), calls=%async_computation.7 | async-start | bytes 1179648 | tf_op jit(solution)/shard_map/all_gather | solution.py:279
  213.0 9.2 %copy-start.7 = (s32[1,1,2,2048]{3,2,1,0:T(2,128)S(1)}, s32[1,1,2,2048]{3,2,1,0:T(2,128)}, u32[]{:S(2)}) copy-start(s32[1,1,2,2048]{3,2,1,0:T(2,128)} %param.23) | copy-start | bytes 49156
  213.0 12.0 %copy-start.8 = (s32[1,1,2048]{2,1,0:T(1,128)S(1)}, s32[1,1,2048]{2,1,0:T(1,128)}, u32[]{:S(2)}) copy-start(s32[1,1,2048]{2,1,0:T(1,128)} %param.21) | copy-start | bytes 24580
  222.2 5.4 %copy-start.1 = (f32[8,80,1024]{2,1,0:T(8,128)S(1)}, f32[8,80,1024]{2,1,0:T(8,128)}, u32[]{:S(2)}) copy-start(f32[8,80,1024]{2,1,0:T(8,128)} %advect.2) | copy-start | bytes 7864324
Sparse Core Ops, SparseCore 0:
  9.9 32.8 all-gather.5
  44.7 30.4 all-gather.7
  77.1 38.5 all-gather.9
  117.4 30.2 all-gather.11
  222.4 26.4 all-gather.13
where the time goes:
time: 276 us; the launch traced here: 275 us
  Pallas kernels  115 us (42%)
  matrix products  42.1 us (15%)
  waiting for transfers between devices  33.4 us (12%)
  blocking collectives  22.1 us (8%)
  local copies, waits for them, and re-layouts  19 us (7%)
  starting transfers between devices  14.8 us (5%)
  between operations  14.6 us (5%)
  other arithmetic  13.6 us (5%)
    pallas_call x2, Pallas kernels, advect(): pl.pallas_call(functools.partial(advect_kernel, rows, chunk), grid=(pl.cd...  95.7 us
    dot_general x4, matrix products, contract(): lax.dot_general(weights, operand, (((0,), (0,)), ((), ())), preferred_ele...  32.9 us
    all_to_all x1, blocking collectives, on_device(): lax.all_to_all(piece.astype(jnp.float16), 'comp', split_axis=0, concat_ax...  22.1 us
    all_gather x1, waiting for transfers between devices, on_device(): group = lax.all_gather(profile, 'comp', axis=1, tiled=True)  16.8 us
    pallas_call x1, Pallas kernels, ocean(): pl.pallas_call(ocean_kernel, out_shape=jax.ShapeDtypeStruct((layers, slot...  10.6 us
    ppermute x1, waiting for transfers between devices, on_device(): halo_up = lax.ppermute(edge(spectrum[:, rows - margin:]), 'lat', up)  9.7 us
    dot_general x1, matrix products, on_device(): lax.dot_general(stokes_kernel, own + delta, (((0,), (0,)), ((), ())), pre...  9.18 us
    pallas_call x1, Pallas kernels, finish(): pl.pallas_call(functools.partial(finish_kernel, rows), grid=(pl.cdiv(comp...  9.07 us
  transfers between devices with their start and end apart: 9, of which 3 were waited for; matrix products, arithmetic and copies ran while one was open for 22% of the time, Pallas kernels for 39%

commit v1 on v0

--- a/solution.py
+++ b/solution.py
@@ -17,131 +17,223 @@
 
 def half_limited(b, f):
     t = b * (1.0 / 6.0) + f * (1.0 / 3.0)
-    low = jnp.minimum(jnp.minimum(b, f), t)
-    high = jnp.maximum(jnp.maximum(b, f), t)
-    return jnp.maximum(low, 0.0) + jnp.minimum(high, 0.0)
-
-
-def advect_kernel(rows, chunk, x_ref, up_ref, dn_ref, mask_ref, cour_ref, band_ref, a_s, b_s, u_s, x_s):
+    low = jnp.minimum(jnp.maximum(b, f), 0.0)
+    high = jnp.maximum(jnp.minimum(b, f), 0.0)
+    return jnp.minimum(jnp.maximum(t, low), high)
+
+
+def lane_blocks(ways):
+    lane = lax.broadcasted_iota(jnp.int32, (8, LANES), 1)
+    width = LANES // ways
+    return lane, lane // width, lane % width
+
+
+def spread(natural):
+    ways = len(natural)
+    _, block, at = lane_blocks(ways)
+    picked = [
+        jnp.take_along_axis(x, at * ways + (block + (ways - j)) % ways, axis=1)
+        for j, x in enumerate(natural)
+    ]
+    out = []
+    for v in range(ways):
+        z = picked[-v % ways]
+        for k in range(1, ways):
+            z = jnp.where(block == k, picked[(k - v) % ways], z)
+        out.append(pltpu.roll(z, LANES - v * (LANES // ways), 1) if v else z)
+    return out
+
+
+def gather_back(parts):
+    ways = len(parts)
+    lane, block, _ = lane_blocks(ways)
+    width = LANES // ways
+    turned = [pltpu.roll(x, v * width, 1) if v else x for v, x in enumerate(parts)]
+    out = []
+    for j in range(ways):
+        y = turned[-j % ways]
+        for k in range(1, ways):
+            y = jnp.where(block == k, turned[(k - j) % ways], y)
+        index = (lane % ways + j) % ways * width + lane // ways
+        out.append(jnp.take_along_axis(y, index, axis=1))
+    return out
+
+
+def speeds(column):
+    c = jnp.broadcast_to(column, (8, LANES))
+    return c, jnp.abs(c), c > 0.0
+
+
+def lon_row(e, sea, speed):
+    c, a, pos = speed
+    ways = len(e)
+    nxt = e[1:] + [pltpu.roll(e[0], LANES - 1, 1)]
+    d = [n - x for n, x in zip(nxt, e)]
+    before = [pltpu.roll(d[-1], 1, 1)] + d[:-1]
+    after = d[1:] + [pltpu.roll(d[0], LANES - 1, 1)]
+    flux = [
+        c * jnp.where(pos, e[v], nxt[v]) + a * half_limited(jnp.where(pos, before[v], after[v]), d[v])
+        for v in range(ways)
+    ]
+    behind = [pltpu.roll(flux[-1], 1, 1)] + flux[:-1]
+    return [sea[v] * (e[v] - (flux[v] - behind[v])) for v in range(ways)]
+
+
+def parts_of(row):
+    return [row[:, j * LANES : (j + 1) * LANES] for j in range(row.shape[1] // LANES)]
+
+
+def first_kernel(rows, x_ref, mask_ref, cour_ref, out_ref, x_s):
     lon = x_ref.shape[1]
+    ways = lon // LANES
+    for t in range(x_ref.shape[0] // 8):
+        tile = spread([x_ref[t * 8 : t * 8 + 8, j * LANES : (j + 1) * LANES] for j in range(ways)])
+        for v in range(ways):
+            x_s[v, t * 8 : t * 8 + 8, :] = tile[v]
+
+    @pl.loop(0, CB // 8)
+    def _(half):
+        base = pl.multiple_of(half * 8, 8)
+        speed = speeds(cour_ref[pl.ds(base, 8), 0:1])
+        for r in range(rows):
+            sea = parts_of(mask_ref[r : r + 1, :])
+            e = [x_s[v, pl.ds(half * (8 * rows) + r, 8, stride=rows), :] * sea[v] for v in range(ways)]
+            out = lon_row(e, sea, speed)
+            for v in range(ways):
+                out_ref[r, pl.ds(base, 8), v * LANES : (v + 1) * LANES] = out[v]
+
+
+def first_sweep(spectrum, mask_rows, cour):
+    comps, rows, lon = spectrum.shape
+    return pl.pallas_call(
+        functools.partial(first_kernel, rows),
+        grid=(pl.cdiv(comps, CB),),
+        in_specs=[
+            pl.BlockSpec((CB * rows, lon), lambda i: (i, 0)),
+            pl.BlockSpec((rows, lon), lambda i: (0, 0)),
+            pl.BlockSpec((CB, 2), lambda i: (i, 0)),
+        ],
+        out_specs=pl.BlockSpec((rows, CB, lon), lambda i: (0, i, 0)),
+        out_shape=jax.ShapeDtypeStruct((rows, comps, lon), jnp.float32),
+        scratch_shapes=[pltpu.VMEM((lon // LANES, CB * rows, LANES), jnp.float32)],
+        cost_estimate=pl.CostEstimate(
+            flops=comps * rows * lon * 400, bytes_accessed=comps * rows * lon * 8, transcendentals=0
+        ),
+        name="first_sweep",
+    )(spectrum.reshape(comps * rows, lon), mask_rows, cour)
+
+
+def advect_kernel(rows, chunk, x_ref, up_ref, dn_ref, mask_ref, cour_ref, band_ref, a_s, b_s, u_s):
+    lon = x_ref.shape[2]
+    ways = lon // LANES
     margin = 2 * ADV
     total = rows + 2 * margin
-    dests = band_ref.shape[0]
-    for j in range(lon // LANES):
-        x_s[j] = x_ref[:, j * LANES : (j + 1) * LANES]
     for r in range(margin):
         u_s[r] = up_ref[r].astype(jnp.float32)
         u_s[margin + r] = dn_ref[r].astype(jnp.float32)
-
-    def wide(column):
-        return jnp.concatenate([jnp.broadcast_to(column, (8, LANES))] * (lon // LANES), axis=1)
 
     @pl.loop(0, CB // 8)
     def _(half):
         base = pl.multiple_of(half * 8, 8)
         cour = cour_ref[pl.ds(base, 8), :]
-        c_lon, c_lat = wide(cour[:, 0:1]), wide(cour[:, 1:2])
-        a_lon, a_lat = jnp.abs(c_lon), jnp.abs(c_lat)
-        pos_lon, pos_lat = c_lon > 0.0, c_lat > 0.0
+        lon_speed = speeds(cour[:, 0:1])
+        c, a, pos = speeds(cour[:, 1:2])
 
         def sea_row(r):
-            return mask_ref[r : r + 1, :]
-
-        def lon_row(e, sea):
-            nxt = pltpu.roll(e, lon - 1, 1)
-            d = nxt - e
-            b = jnp.where(pos_lon, pltpu.roll(d, 1, 1), pltpu.roll(d, lon - 1, 1))
-            flux = c_lon * jnp.where(pos_lon, e, nxt) + a_lon * half_limited(b, d)
-            return sea * (e - (flux - pltpu.roll(flux, 1, 1)))
-
-        def start_row(r):
-            if r < margin:
-                return u_s[r, pl.ds(base, 8), :]
-            if r >= margin + rows:
-                return u_s[r - rows, pl.ds(base, 8), :]
-            first = half * (8 * rows) + (r - margin)
-            return jnp.concatenate(
-                [x_s[j, pl.ds(first, 8, stride=rows), :] for j in range(lon // LANES)], axis=1
-            )
-
-        def store_row(r, value):
-            at = 0
-            while at < lon:
-                d, lane = divmod((r - margin) * lon + at, chunk)
-                n = min(chunk - lane, lon - at)
-                band_ref[d, pl.ds(base, 8), lane : lane + n] = value[:, at : at + n]
-                at += n
+            return parts_of(mask_ref[r : r + 1, :])
+
+        def put(ref, r, value):
+            for v in range(ways):
+                ref[r, :, v * LANES : (v + 1) * LANES] = value[v]
+
+        def swept_row(r):
+            if margin <= r < margin + rows:
+                return parts_of(x_ref[r - margin, pl.ds(base, 8), :])
+            return parts_of(a_s[r])
+
+        for k in range(2 * margin):
+            r = k if k < margin else rows + k
+            sea = sea_row(r)
+            e = spread(parts_of(u_s[k, pl.ds(base, 8), :]))
+            put(a_s, r, lon_row([e[v] * sea[v] for v in range(ways)], sea, lon_speed))
 
         for substep in range(ADV):
             gone = 2 * substep
-            for r in range(gone, total - gone):
-                sea = sea_row(r)
-                e = start_row(r) * sea if substep == 0 else b_s[r]
-                a_s[r] = lon_row(e, sea)
-            cur, nxt = a_s[gone], a_s[gone + 1]
-            d = nxt - cur
-            dm, before = d, None
-            for r in range(gone + 1, total - gone - 2):
-                cur, nxt, dm = nxt, a_s[r + 1], d
-                d = nxt - cur
-                dp = a_s[r + 2] - nxt
-                b = jnp.where(pos_lat, dm, dp)
-                flux = c_lat * jnp.where(pos_lat, cur, nxt) + a_lat * half_limited(b, d)
-                if before is not None:
-                    value = sea_row(r) * (cur - (flux - before))
-                    if substep == ADV - 1:
-                        store_row(r, value)
-                    else:
-                        b_s[r] = value
-                before = flux
-
-
-def advect(spectrum, halo_up, halo_dn, mask_rows, cour, dests, first, size):
-    comps, rows, lon = spectrum.shape
+            row = swept_row
+            if substep:
+                for r in range(gone, total - gone):
+                    put(a_s, r, lon_row(parts_of(b_s[r]), sea_row(r), lon_speed))
+                row = lambda r: parts_of(a_s[r])
+            for v in range(ways):
+                cur, nxt = row(gone)[v], row(gone + 1)[v]
+                d, fl = nxt - cur, None
+                ahead = row(gone + 2)[v]
+                dp = ahead - nxt
+                for r in range(gone + 1, total - gone - 2):
+                    cur, nxt, dm, d = nxt, ahead, d, dp
+                    ahead = row(r + 2)[v]
+                    dp = ahead - nxt
+                    now = c * jnp.where(pos, cur, nxt) + a * half_limited(jnp.where(pos, dm, dp), d)
+                    if fl is not None:
+                        value = sea_row(r)[v] * (cur - (now - fl))
+                        if substep == ADV - 1:
+                            at = (r - margin) * lon + v * LANES
+                            to, lane = divmod(at, chunk)
+                            band_ref[to, pl.ds(base, 8), lane : lane + LANES] = value
+                        else:
+                            b_s[r, :, v * LANES : (v + 1) * LANES] = value
+                    fl = now
+
+
+def advect(swept, halo_up, halo_dn, mask_rows, cour, dests, first, size):
+    rows, comps, lon = swept.shape
     chunk = rows * lon // dests
     margin = 2 * ADV
     skip = first // CB
     total = rows + 2 * margin
-    blk = pl.BlockSpec((dests, CB, chunk), lambda i: (0, i, 0))
     return pl.pallas_call(
         functools.partial(advect_kernel, rows, chunk),
         grid=(pl.cdiv(size, CB),),
         in_specs=[
-            pl.BlockSpec((CB * rows, lon), lambda i: (i + skip, 0)),
+            pl.BlockSpec((rows, CB, lon), lambda i: (0, i + skip, 0)),
             pl.BlockSpec((margin, CB, lon), lambda i: (0, i + skip, 0)),
             pl.BlockSpec((margin, CB, lon), lambda i: (0, i + skip, 0)),
             pl.BlockSpec((total, lon), lambda i: (0, 0)),
             pl.BlockSpec((CB, 2), lambda i: (i + skip, 0)),
         ],
-        out_specs=blk,
+        out_specs=pl.BlockSpec((dests, CB, chunk), lambda i: (0, i, 0)),
         out_shape=jax.ShapeDtypeStruct((dests, size, chunk), jnp.float32),
         scratch_shapes=[
             pltpu.VMEM((total, 8, lon), jnp.float32),
             pltpu.VMEM((total, 8, lon), jnp.float32),
             pltpu.VMEM((2 * margin, CB, lon), jnp.float32),
-            pltpu.VMEM((lon // LANES, CB * rows, LANES), jnp.float32),
         ],
         cost_estimate=pl.CostEstimate(
             flops=size * rows * lon * 400, bytes_accessed=size * rows * lon * 8, transcendentals=0
         ),
         name="advect",
-    )(spectrum.reshape(comps * rows, lon), halo_up, halo_dn, mask_rows, cour)
+    )(swept, halo_up, halo_dn, mask_rows, cour)
 
 
 def finish_kernel(rows, band_ref, delta_ref, out_ref, o_s):
     dests, cb, chunk = band_ref.shape
     lon = out_ref.shape[1]
-    for d in range(dests):
-        at = 0
-        while at < chunk:
-            point = d * chunk + at
-            r, lane = point // lon, point % lon
-            n = min(lon - lane, chunk - at)
-            v = band_ref[d, :, at : at + n] + delta_ref[d, :, at : at + n].astype(jnp.float32)
-            for j in range(n // LANES):
-                o_s[lane // LANES + j, pl.ds(r, cb, stride=rows), :] = v[:, j * LANES : (j + 1) * LANES]
-            at += n
-    for j in range(lon // LANES):
+    ways = lon // LANES
+    for r in range(rows):
+        for h in range(0, cb, 8):
+            v = []
+            for j in range(ways):
+                d, at = divmod(r * lon + j * LANES, chunk)
+                pick = (d, slice(h, h + 8), slice(at, at + LANES))
+                v.append(band_ref[pick])
+            w = []
+            for j in range(ways):
+                d, at = divmod(r * lon + j * LANES, chunk)
+                w.append(delta_ref[d, :, at : at + LANES].astype(jnp.float32)[h : h + 8])
+            back = gather_back([x + y for x, y in zip(v, w)])
+            for j in range(ways):
+                o_s[j, pl.ds(h * rows + r, 8, stride=rows), :] = back[j]
+    for j in range(ways):
         out_ref[:, j * LANES : (j + 1) * LANES] = o_s[j]
 
 
@@ -247,6 +339,8 @@
     bands, dests = lax.axis_size("lat"), lax.axis_size("comp")
     band_index = lax.axis_index("lat")
     sea = jnp.pad(mask.astype(jnp.float32), ((margin, margin), (0, 0)))
+    ways = lon // LANES
+    sea = sea.reshape(-1, LANES, ways).transpose(0, 2, 1).reshape(-1, lon)
     mask_rows = lax.dynamic_slice_in_dim(sea, band_index * rows, rows + 2 * margin, 0)
     up = [(i, i + 1) for i in range(bands - 1)]
     down = [(j, i) for i, j in up]
@@ -257,11 +351,13 @@
     halo_up = lax.ppermute(edge(spectrum[:, rows - margin :]), "lat", up)
     halo_dn = lax.ppermute(edge(spectrum[:, :margin]), "lat", down)
     weights = [lax.all_gather(w, "comp", axis=0, tiled=True) for w in (proj_a, proj_b, proj_c, proj_d)]
+    cour = courant.T
+    swept = first_sweep(spectrum, mask_rows[margin : margin + rows], cour)
     bands_of, points_of = [], []
     width = pl.cdiv(pl.cdiv(comps, CB), PIECES) * CB
     for first in range(0, comps, width):
         piece = advect(
-            spectrum, halo_up, halo_dn, mask_rows, courant.T, dests, first, min(width, comps - first)
+            swept, halo_up, halo_dn, mask_rows, cour, dests, first, min(width, comps - first)
         )
         bands_of.append(piece)
         points_of.append(lax.all_to_all(piece.astype(jnp.float16), "comp", split_axis=0, concat_axis=0))
@@ -280,7 +376,10 @@
     back = lax.all_to_all(
         delta.astype(jnp.bfloat16).reshape(dests, comps, chunk), "comp", split_axis=0, concat_axis=0
     )
-    force = ocean(group, tile_points[0, 0], tile_counts[0, 0], tile_nbr[0, 0], vorticity[0, 0], diffusivity[0, 0])
+    where = tile_points[0, 0]
+    cell = where % lon
+    where = where - cell + cell % ways * LANES + cell // ways
+    force = ocean(group, where, tile_counts[0, 0], tile_nbr[0, 0], vorticity[0, 0], diffusivity[0, 0])
     return finish(band, back, rows, lon), force[None, None]
 
 

time: 276 us -> 246 us (0.89)
  Pallas kernels: 115 us -> 71.1 us
  waiting for transfers between devices: 33.4 us -> 42.4 us
    pallas_call x2, Pallas kernels: 95.7 us -> 20.5 us  [advect(): pl.pallas_call(functools.partial(advect_kernel, rows, chunk), grid=(pl.cd...]
    pallas_call x0 -> x1, Pallas kernels: none -> 21.7 us  [first_sweep(): pl.pallas_call(functools.partial(first_kernel, rows), grid=(pl.cdiv(comps...]
    all_gather x4, waiting for transfers between devices: 0.03 us -> 15.3 us  [on_device(): lax.all_gather(w, 'comp', axis=0, tiled=True)]
    ppermute x1, waiting for transfers between devices: 9.7 us -> 0.01 us  [on_device(): halo_up = lax.ppermute(edge(spectrum[:, rows - margin:]), 'lat', up)]
    pallas_call x1, Pallas kernels: 9.07 us -> 18.3 us  [finish(): pl.pallas_call(functools.partial(finish_kernel, rows), grid=(pl.cdiv(comp...]
    all_to_all x1, waiting for transfers between devices: 0.01 us -> 8.68 us  [on_device(): lax.all_to_all(piece.astype(jnp.float16), 'comp', split_axis=0, concat_ax...]
    ppermute x1, waiting for transfers between devices: 4.26 us -> 0.01 us  [on_device(): halo_dn = lax.ppermute(edge(spectrum[:, :margin]), 'lat', down)]
    add x0 -> x1, other arithmetic: none -> 3.58 us  [on_device(): where = where - cell + cell % ways * LANES + cell // ways]
  transfers between devices with their start and end apart: 9 -> 9, of which waited for: 3 -> 3; matrix products, arithmetic and copies ran while one was open for 22% -> 26% of each run, Pallas kernels for 39% -> 21%
where the time goes in v1:
time: 246 us
  Pallas kernels  71.1 us (29%)
  waiting for transfers between devices  42.4 us (17%)
  matrix products  42.1 us (17%)
  blocking collectives  24.1 us (10%)
  local copies, waits for them, and re-layouts  21 us (9%)
  other arithmetic  15.4 us (6%)
  starting transfers between devices  14.8 us (6%)
  between operations  14.8 us (6%)
    dot_general x4, matrix products, contract(): lax.dot_general(weights, operand, (((0,), (0,)), ((), ())), preferred_ele...  32.9 us
    all_to_all x1, blocking collectives, on_device(): lax.all_to_all(piece.astype(jnp.float16), 'comp', split_axis=0, concat_ax...  24.1 us
    pallas_call x1, Pallas kernels, first_sweep(): pl.pallas_call(functools.partial(first_kernel, rows), grid=(pl.cdiv(comps...  21.7 us
    pallas_call x2, Pallas kernels, advect(): pl.pallas_call(functools.partial(advect_kernel, rows, chunk), grid=(pl.cd...  20.5 us
    pallas_call x1, Pallas kernels, finish(): pl.pallas_call(functools.partial(finish_kernel, rows), grid=(pl.cdiv(comp...  18.3 us
    all_gather x1, waiting for transfers between devices, on_device(): group = lax.all_gather(profile, 'comp', axis=1, tiled=True)  15.7 us
    all_gather x4, waiting for transfers between devices, on_device(): lax.all_gather(w, 'comp', axis=0, tiled=True)  15.3 us
    pallas_call x1, Pallas kernels, ocean(): pl.pallas_call(ocean_kernel, out_shape=jax.ShapeDtypeStruct((layers, slot...  10.6 us
  transfers between devices with their start and end apart: 9, of which 3 were waited for; matrix products, arithmetic and copies ran while one was open for 26% of the time, Pallas kernels for 21%

profile of v1, /device:TPU:0, one launch (start us, length us, event | category | flops | bytes accessed | tf_op | source)
XLA Modules:
  0.0 245.8 jit_solution(13797245061521903793)
XLA Ops:
  7.2 0.7 all-gather.6.cloned.1.call-update
  7.9 0.0 all-gather.8.cloned.1.call-start
  8.0 0.7 all-gather.8.cloned.1.call-update
  8.7 0.0 all-gather.10.cloned.1.call-start
  8.7 0.7 all-gather.10.cloned.1.call-update
  9.4 3.0 %fusion.21 = (bf16[144,4,512]{2,1,0:T(4,128)(2,1)S(1)}, bf16[144,4,512]{2,1,0:T(4,128)(2,1)S(1)}) fusion(f32[144,16,512]{2,1,0:T(8,128)} %param.13), kind=kLoop, calls=%fused_computation.39 | loop fusion | bytes 2359296 | tf_op jit(solution)/shard_map/slice | solution.py:352
  12.4 0.1 copy.50
  12.5 5.0 %collective-permute-start = (bf16[4,144,512]{2,1,0:T(8,128)(2,1)S(1)}, bf16[4,144,512]{2,1,0:T(8,128)(2,1)S(1)}, u32[]{:S(2)}, u32[]{:S(2)}) collective-permute-start(bf16[4,144,512]{2,1,0:T(8,128)(2,1)S(1)} %bitcast.59), channel_id=1, source_target_pairs={{0,8},{8,16},{16,24},{1,9},{9,17},{17,25},{2,10},{10,18},{18,26},{... | collective-permute-start | bytes 1769480 | tf_op jit(solution)/shard_map/ppermute | solution.py:351
  17.5 0.1 copy.51
  17.6 1.3 collective-permute-start.1
  19.0 0.1 copy.52
  19.1 0.1 pad.4.clone
  19.2 0.1 copy.37
  19.4 0.7 copy.38
  20.1 0.6 constant_dynamic-slice_fusion.mask_ref
  20.8 21.7 %first_sweep.1.x_ref = f32[16,144,512]{2,1,0:T(8,128)} custom-call(f32[2304,512]{1,0:T(8,128)} %bitcast.52, f32[16,512]{1,0:T(8,128)} %constant_dynamic-slice_fusion.mask_ref, f32[144,2]{1,0:T(8,128)} %bitcast.54), custom_call_target="tpu_custom_call" | custom-call | flops 471859200 | bytes 9437184 | tf_op jit(solution)/shard_map/first_sweep/pallas_call | solution.py:108
  42.5 0.6 constant_dynamic-slice_fusion.1.mask_ref
  43.1 0.8 copy-done.4
  43.9 0.8 copy-done.5
  44.7 9.3 %advect.3 = f32[8,64,1024]{2,1,0:T(8,128)} custom-call(f32[16,144,512]{2,1,0:T(8,128)} %first_sweep.1.x_ref, bf16[4,144,512]{2,1,0:T(8,128)(2,1)} %copy-done.4, bf16[4,144,512]{2,1,0:T(8,128)(2,1)} %copy-done.5, f32[24,512]{1,0:T(8,128)} %constant_dynamic-slice_fusion.1.mask_ref, f32[144,2]{1,0:T(8,128)} %bitcast.55), custom_call_target="tpu_custom_call" | custom-call | flops 209715200 | bytes 4194304 | tf_op jit(solution)/shard_map/advect/pallas_call | solution.py:194
  54.1 2.7 %convert_element_type.53 = f16[8,64,1024]{2,1,0:T(8,128)(2,1)} convert(f32[8,64,1024]{2,1,0:T(8,128)} %advect.3) | non-fusion elementwise | flops 524288 | bytes 3145728 | tf_op jit(solution)/shard_map/convert_element_type | solution.py:363
  56.8 3.7 %all-to-all-start.1 = ((f16[8,64,1024]{2,1,0:T(8,128)(2,1)}), f16[8,64,1024]{2,1,0:T(8,128)(2,1)S(1)}, u32[]{:S(2)}, u32[]{:S(2)}) async-start(f16[8,64,1024]{2,1,0:T(8,128)(2,1)} %convert_element_type.53), calls=%async_computation.1 | async-start | bytes 2097152 | tf_op jit(solution)/shard_map/all_to_all | solution.py:363
  60.6 0.5 all-gather.12.cloned.1.call-update
  61.1 11.2 %advect.2 = f32[8,80,1024]{2,1,0:T(8,128)} custom-call(f32[16,144,512]{2,1,0:T(8,128)} %first_sweep.1.x_ref, bf16[4,144,512]{2,1,0:T(8,128)(2,1)} %copy-done.4, bf16[4,144,512]{2,1,0:T(8,128)(2,1)} %copy-done.5, f32[24,512]{1,0:T(8,128)} %constant_dynamic-slice_fusion.1.mask_ref, f32[144,2]{1,0:T(8,128)} %bitcast.56), custom_call_target="tpu_custom_call" | custom-call | flops 262144000 | bytes 5242880 | tf_op jit(solution)/shard_map/advect/pallas_call | solution.py:194
  72.3 2.0 convert_element_type.52
  74.3 8.7 %all-to-all-done.1 = f16[8,64,1024]{2,1,0:T(8,128)(2,1)S(1)} async-done(((f16[8,64,1024]{2,1,0:T(8,128)(2,1)}), f16[8,64,1024]{2,1,0:T(8,128)(2,1)S(1)}, u32[]{:S(2)}, u32[]{:S(2)}) %all-to-all-start.1) | async-done | bytes 1048608 | tf_op jit(solution)/shard_map/all_to_all | solution.py:363
  83.0 24.1 %all_to_all.15 = f16[8,80,1024]{2,1,0:T(8,128)(2,1)S(1)} all-to-all(f16[8,80,1024]{2,1,0:T(8,128)(2,1)S(1)} %convert_element_type.52), channel_id=1, replica_groups=mesh['lat'=4,'comp'=8] {'comp'}, dimensions={0} | all-to-all | bytes 2621440 | tf_op jit(solution)/shard_map/all_to_all | solution.py:363
  107.1 0.7 pad_maximum_fusion.1
  107.8 3.2 %fusion.5 = (bf16[1152,1024]{1,0:T(8,128)(2,1)S(1)}, f32[1152,1024]{1,0:T(8,128)}) fusion(f16[8,144,1024]{2,1,0:T(8,128)(2,1)S(1)} %pad_maximum_fusion.1), kind=kLoop, calls=%fused_computation.18 | loop fusion | flops 2359296 | bytes 9437184 | tf_op jit(solution)/shard_map/convert_element_type | solution.py:369
  111.0 7.2 %copy.41 = f32[1152,1024]{0,1:T(8,128)} copy(f32[1152,1024]{1,0:T(8,128)} %get-tuple-element.5) | data formatting | bytes 9437184 | tf_op jit(solution)/shard_map/convert_element_type | solution.py:368
  118.2 7.0 %fusion.23 = f32[1024,1152]{1,0:T(8,128)} fusion(bf16[1152,1024]{1,0:T(8,128)(2,1)S(1)} %get-tuple-element.4, bf16[1152,1152]{1,0:T(8,128)(2,1)} %all-gather.6.cloned.1.call-done), kind=kOutput, calls=%fused_computation.41 | convolution fusion | flops 2717908992 | bytes 9732096 | tf_op jit(solution)/shard_map/dot_general | solution.py:317
  125.1 7.4 %fusion.4 = bf16[1024,1152]{1,0:T(8,128)(2,1)S(1)} fusion(f32[1024,1152]{1,0:T(8,128)} %fusion.23, bf16[1152,1024]{1,0:T(8,128)(2,1)} %copy-done.6, bf16[1152,1152]{1,0:T(8,128)(2,1)} %all-gather.8.cloned.1.call-done), kind=kOutput, calls=%fused_computation.7 | convolution fusion | flops 2720268288 | bytes 12091392 | tf_op jit(solution)/shard_map/dot_general | solution.py:317
  132.6 7.7 %fusion.24 = f32[1024,1152]{1,0:T(8,128)} fusion(bf16[1024,1152]{1,0:T(8,128)(2,1)S(1)} %fusion.4, bf16[1152,1152]{1,0:T(8,128)(2,1)} %all-gather.10.cloned.1.call-done), kind=kOutput, calls=%fused_computation.42 | convolution fusion | flops 2717908992 | bytes 9732096 | tf_op jit(solution)/shard_map/dot_general | solution.py:317
  140.3 15.3 %all-gather.12.cloned.1.call-done = bf16[1152,1152]{1,0:T(8,128)(2,1)} async-done(((bf16[144,1152]{1,0:T(8,128)(2,1)}), bf16[1152,1152]{1,0:T(8,128)(2,1)}) %all-gather.12.cloned.1.call-update) | async-done | bytes 2654224 | tf_op jit(solution)/shard_map/all_gather | solution.py:353
  155.6 10.9 %fusion.22 = (bf16[1152,1024]{0,1:T(8,128)(2,1)S(1)}, f32[1152,1024]{0,1:T(8,128)}) fusion(f32[1152,1024]{0,1:T(8,128)} %copy.41, bf16[1024,1152]{1,0:T(8,128)(2,1)} %copy-done.3, bf16[1152,1152]{1,0:T(8,128)(2,1)} %all-gather.12.cloned.1.call-done, f32[1024,1152]{1,0:T(8,128)} %fusion.24), kind=kOutput, calls=%fused_computation.40 | convolution fusion | flops 2722627584 | bytes 21528576 | tf_op jit(solution)/shard_map/dot_general | solution.py:317
  166.5 2.5 %copy.42 = bf16[1152,1024]{1,0:T(8,128)(2,1)} copy(bf16[1152,1024]{0,1:T(8,128)(2,1)S(1)} %get-tuple-element.8) | data formatting | bytes 4718592 | tf_op jit(solution)/shard_map/convert_element_type | solution.py:377
  169.0 4.4 %all-to-all-start.2 = ((bf16[8,144,1024]{2,1,0:T(8,128)(2,1)}), bf16[8,144,1024]{2,1,0:T(8,128)(2,1)}, u32[]{:S(2)}, u32[]{:S(2)}) async-start(bf16[8,144,1024]{2,1,0:T(8,128)(2,1)} %bitcast.51), calls=%async_computation.2 | async-start | bytes 4718592 | tf_op jit(solution)/shard_map/all_to_all | solution.py:376
  173.4 0.3 all-gather.14.cloned.1.call-start
  173.7 9.2 %fusion.9 = bf16[64,1024]{1,0:T(8,128)(2,1)} fusion(f32[1152,64]{0,1:T(8,128)S(1)} %copy-done, f32[1152,1024]{0,1:T(8,128)} %copy.41, f32[1152,1024]{0,1:T(8,128)} %get-tuple-element.9), kind=kOutput, calls=%fused_computation.20 | convolution fusion | flops 907214848 | bytes 9863168 | tf_op jit(solution)/shard_map/dot_general | solution.py:372
  182.9 1.4 copy.48.east_ref
  184.3 1.4 copy.49.north_ref
  185.7 1.3 copy.47
  187.8 0.6 compare_convert_fusion.live_ref
  188.4 3.6 %fusion.15.pts_ref = s32[2048,1]{1,0:T(8,128)} fusion(s32[2048,1]{1,0:T(8,128)} %copy.47), kind=kLoop, calls=%fused_computation.24 | loop fusion | flops 69632 | bytes 16384 | tf_op jit(solution)/shard_map/add | solution.py:381
  192.0 2.5 %pad_maximum_fusion.band_ref = f32[8,144,1024]{2,1,0:T(8,128)} fusion(f32[8,64,1024]{2,1,0:T(8,128)S(1)} %copy-done.2, f32[8,80,1024]{2,1,0:T(8,128)S(1)} %copy-done.1), kind=kLoop, calls=%fused_computation.1 | loop fusion | flops 1179648 | bytes 9437184 | tf_op jit(solution)/shard_map/concatenate | solution.py:364
  194.5 15.7 %all-gather.14.cloned.1.call-done.prof_ref = bf16[64,8192]{1,0:T(8,128)(2,1)} async-done(((bf16[64,1024]{1,0:T(8,128)(2,1)}), bf16[64,8192]{1,0:T(8,128)(2,1)}) %all-gather.14.cloned.1.call-update) | async-done | bytes 1048592 | tf_op jit(solution)/shard_map/all_gather | solution.py:375
  210.3 10.6 %ocean.1 = f32[64,2048]{1,0:T(8,128)} custom-call(bf16[64,8192]{1,0:T(8,128)(2,1)} %all-gather.14.cloned.1.call-done.prof_ref, s32[2048,1]{1,0:T(8,128)} %fusion.15.pts_ref, s32[2048,1]{1,0:T(8,128)} %copy.48.east_ref, s32[2048,1]{1,0:T(8,128)} %copy.49.north_ref, f32[1,2048]{1,0:T(1,128)} %compare_convert_fusion.live_ref, f32[64,2048]{1,0:T(8,128)} %bitcast.61, ...), custom_call_target="tpu_custom_call" | custom-call | tf_op jit(solution)/shard_map/ocean/pallas_call | solution.py:305
  220.9 18.3 %finish.1 = f32[2304,512]{1,0:T(8,128)} custom-call(f32[8,144,1024]{2,1,0:T(8,128)} %pad_maximum_fusion.band_ref, bf16[8,144,1024]{2,1,0:T(8,128)(2,1)} %all-to-all-done.2.delta_ref), custom_call_target="tpu_custom_call" | custom-call | tf_op jit(solution)/shard_map/finish/pallas_call | solution.py:243
  (32 shorter events, 0.2 us)
Async XLA Ops:
  7.2 166.5 %copy-start = (f32[1152,64]{0,1:T(8,128)S(1)}, f32[1152,64]{0,1:T(8,128)}, u32[]{:S(2)}) copy-start(f32[1152,64]{0,1:T(8,128)} %param.20) | copy-start | bytes 884740
  7.2 111.0 %all-gather.6.cloned.1.call-start = ((), (), s32[]{:S(2)}) async-start(), calls=%async_computation.3 | async-start | bytes 2985984 | tf_op jit(solution)/shard_map/all_gather | solution.py:353
  7.9 11.0 %copy-start.7 = (s32[64,512]{1,0:T(8,128)S(1)}, s32[64,512]{1,0:T(8,128)}, u32[]{:S(2)}) copy-start(s32[64,512]{1,0:T(8,128)} %param.14) | copy-start | bytes 393220
  7.9 117.2 %all-gather.8.cloned.1.call-start = ((), (), s32[]{:S(2)}) async-start(), calls=%async_computation.4 | async-start | bytes 2985984 | tf_op jit(solution)/shard_map/all_gather | solution.py:353
  8.7 123.9 %all-gather.10.cloned.1.call-start = ((), (), s32[]{:S(2)}) async-start(), calls=%async_computation.5 | async-start | bytes 2985984 | tf_op jit(solution)/shard_map/all_gather | solution.py:353
  12.4 7.0 %copy-start.10 = (f32[2,144]{1,0:T(2,128)S(1)}, f32[2,144]{1,0:T(2,128)}, u32[]{:S(2)}) copy-start(f32[2,144]{1,0:T(2,128)} %param.15) | copy-start | bytes 3460
  12.5 30.6 %collective-permute-start = (bf16[4,144,512]{2,1,0:T(8,128)(2,1)S(1)}, bf16[4,144,512]{2,1,0:T(8,128)(2,1)S(1)}, u32[]{:S(2)}, u32[]{:S(2)}) collective-permute-start(bf16[4,144,512]{2,1,0:T(8,128)(2,1)S(1)} %bitcast.59), channel_id=1, source_target_pairs={{0,8},{8,16},{16,24},{1,9},{9,17},{17,25},{2,10},{10,18},{18,26},{... | collective-permute-start | bytes 1769480 | tf_op jit(solution)/shard_map/ppermute | solution.py:351
  17.6 25.5 %collective-permute-start.1 = (bf16[4,144,512]{2,1,0:T(8,128)(2,1)S(1)}, bf16[4,144,512]{2,1,0:T(8,128)(2,1)S(1)}, u32[]{:S(2)}, u32[]{:S(2)}) collective-permute-start(bf16[4,144,512]{2,1,0:T(8,128)(2,1)S(1)} %bitcast.60), channel_id=1, source_target_pairs={{8,0},{16,8},{24,16},{9,1},{17,9},{25,17},{10,2},{18,10},{26,18},{... | collective-permute-start | bytes 1769480 | tf_op jit(solution)/shard_map/ppermute | solution.py:352
  43.1 0.8 copy-start.4
  43.9 0.8 copy-start.5
  56.8 26.2 %all-to-all-start.1 = ((f16[8,64,1024]{2,1,0:T(8,128)(2,1)}), f16[8,64,1024]{2,1,0:T(8,128)(2,1)S(1)}, u32[]{:S(2)}, u32[]{:S(2)}) async-start(f16[8,64,1024]{2,1,0:T(8,128)(2,1)} %convert_element_type.53), calls=%async_computation.1 | async-start | bytes 2097152 | tf_op jit(solution)/shard_map/all_to_all | solution.py:363
  60.5 95.1 %all-gather.12.cloned.1.call-start = ((), (), s32[]{:S(2)}) async-start(), calls=%async_computation.6 | async-start | bytes 2985984 | tf_op jit(solution)/shard_map/all_gather | solution.py:353
  111.0 7.2 %copy-start.6 = (bf16[1152,1024]{1,0:T(8,128)(2,1)}, bf16[1152,1024]{1,0:T(8,128)(2,1)S(1)}, u32[]{:S(2)}) copy-start(bf16[1152,1024]{1,0:T(8,128)(2,1)S(1)} %get-tuple-element.4) | copy-start | bytes 7077892
  132.6 7.7 %copy-start.3 = (bf16[1024,1152]{1,0:T(8,128)(2,1)}, bf16[1024,1152]{1,0:T(8,128)(2,1)S(1)}, u32[]{:S(2)}) copy-start(bf16[1024,1152]{1,0:T(8,128)(2,1)S(1)} %fusion.4) | copy-start | bytes 7077892
  169.0 51.9 %all-to-all-start.2 = ((bf16[8,144,1024]{2,1,0:T(8,128)(2,1)}), bf16[8,144,1024]{2,1,0:T(8,128)(2,1)}, u32[]{:S(2)}, u32[]{:S(2)}) async-start(bf16[8,144,1024]{2,1,0:T(8,128)(2,1)} %bitcast.51), calls=%async_computation.2 | async-start | bytes 4718592 | tf_op jit(solution)/shard_map/all_to_all | solution.py:376
  173.4 36.9 %all-gather.14.cloned.1.call-start = ((), (), s32[]{:S(2)}) async-start(), calls=%async_computation.7 | async-start | bytes 1179648 | tf_op jit(solution)/shard_map/all_gather | solution.py:375
  173.7 9.2 %copy-start.8 = (s32[1,1,2,2048]{3,2,1,0:T(2,128)S(1)}, s32[1,1,2,2048]{3,2,1,0:T(2,128)}, u32[]{:S(2)}) copy-start(s32[1,1,2,2048]{3,2,1,0:T(2,128)} %param.23) | copy-start | bytes 49156
  173.7 12.0 %copy-start.9 = (s32[1,1,2048]{2,1,0:T(1,128)S(1)}, s32[1,1,2048]{2,1,0:T(1,128)}, u32[]{:S(2)}) copy-start(s32[1,1,2048]{2,1,0:T(1,128)} %param.21) | copy-start | bytes 24580
  182.9 9.1 %copy-start.1 = (f32[8,80,1024]{2,1,0:T(8,128)S(1)}, f32[8,80,1024]{2,1,0:T(8,128)}, u32[]{:S(2)}) copy-start(f32[8,80,1024]{2,1,0:T(8,128)} %advect.2) | copy-start | bytes 7864324
  187.0 5.0 %copy-start.2 = (f32[8,64,1024]{2,1,0:T(8,128)S(1)}, f32[8,64,1024]{2,1,0:T(8,128)}, u32[]{:S(2)}) copy-start(f32[8,64,1024]{2,1,0:T(8,128)} %advect.3) | copy-start | bytes 6291460
Sparse Core Ops, SparseCore 0:
  9.9 32.8 all-gather.5
  44.7 37.2 all-gather.7
  83.9 39.7 all-gather.9
  125.5 30.1 all-gather.11
  183.0 27.2 all-gather.13

commit v2 on v0

v2 whole, which is shorter than its diff:
```python
import functools

import jax
import jax.numpy as jnp
from jax import lax
from jax.experimental import pallas as pl
from jax.experimental.pallas import tpu as pltpu
from jax.sharding import PartitionSpec as P

ADV = 2
time_step = 0.25
CB = 16
LANES = 128
LOW = 256
MESH = pl.DeviceIdType.MESH
STEPS = 16000.0


def half_limited(b, f):
    t = b * (1.0 / 6.0) + f * (1.0 / 3.0)
    low = jnp.minimum(jnp.maximum(b, f), 0.0)
    high = jnp.maximum(jnp.minimum(b, f), 0.0)
    return jnp.minimum(jnp.maximum(t, low), high)


def rolled(x, shift):
    return pltpu.roll(x, shift % LANES, 1)


def speeds(column, lon):
    c = jnp.broadcast_to(column, (8, lon))
    return c, jnp.abs(c), c > 0.0


def lon_row(e, sea, speed):
    c, a, pos = speed
    last = e.shape[1] - LANES
    nxt = jnp.concatenate([e[:, LANES:], rolled(e[:, :LANES], -1)], axis=1)
    d = nxt - e
    before = jnp.concatenate([rolled(d[:, last:], 1), d[:, :last]], axis=1)
    after = jnp.concatenate([d[:, LANES:], rolled(d[:, :LANES], -1)], axis=1)
    flux = c * jnp.where(pos, e, nxt) + a * half_limited(jnp.where(pos, before, after), d)
    behind = jnp.concatenate([rolled(flux[:, last:], 1), flux[:, :last]], axis=1)
    return sea * (e - (flux - behind))


def spreader(lon, back=False):
    ways = lon // LANES
    x = lax.broadcasted_iota(jnp.int32, (lon, lon), 1 if back else 0)
    at = lax.broadcasted_iota(jnp.int32, (lon, lon), 0 if back else 1)
    return (x == at % LANES * ways + at // LANES).astype(jnp.bfloat16)


def moved(x, ones):
    high = x.astype(jnp.bfloat16)
    low = (x - high.astype(jnp.float32)).astype(jnp.bfloat16)
    return jnp.dot(high, ones, preferred_element_type=jnp.float32) + jnp.dot(
        low, ones, preferred_element_type=jnp.float32
    )


def flipped(me, bit):
    return me + (1 - 2 * (me // (1 << bit) % 2)) * (1 << bit)


def advect_kernel(
    rows, dests, bands, x_ref, top_ref, end_ref, mask_ref, cour_ref, ones_ref, wa, wb, wc, wd,
    band_ref, pts_ref, ga, gb, gc, gd,
    x_s, swept_s, a_s, b_s, u_s, up_s, dn_s, send_s, own_s,
    halo_send, halo_recv, w_send, w_recv, p_send, p_recv, own_sem,
):
    lon = ones_ref.shape[0]
    chunk = rows * lon // dests
    ways = lon // LANES
    margin = 2 * ADV
    total = rows + 2 * margin
    comps = x_ref.shape[0] // rows
    blocks = comps // CB
    me, lat = lax.axis_index("comp"), lax.axis_index("lat")
    bits = dests.bit_length() - 1
    shards, gathered = (wa, wb, wc, wd), (ga, gb, gc, gd)

    barrier = pltpu.get_barrier_semaphore()
    for k in range(1, dests):
        pl.semaphore_signal(barrier, inc=1, device_id={"comp": (me + k) % dests}, device_id_type=MESH)

    @pl.when(lat + 1 < bands)
    def _():
        pl.semaphore_signal(barrier, inc=1, device_id={"lat": lat + 1}, device_id_type=MESH)

    @pl.when(lat > 0)
    def _():
        pl.semaphore_signal(barrier, inc=1, device_id={"lat": lat - 1}, device_id_type=MESH)

    beside = (lat + bands - 1) // bands + (2 * (bands - 1) - lat) // bands
    pl.semaphore_wait(barrier, dests - 1 + beside)

    def up_copy():
        return pltpu.make_async_remote_copy(
            src_ref=end_ref, dst_ref=up_s, send_sem=halo_send.at[0], recv_sem=halo_recv.at[0],
            device_id={"lat": lat + 1}, device_id_type=MESH,
        )

    def dn_copy():
        return pltpu.make_async_remote_copy(
            src_ref=top_ref, dst_ref=dn_s, send_sem=halo_send.at[1], recv_sem=halo_recv.at[1],
            device_id={"lat": lat - 1}, device_id_type=MESH,
        )

    @pl.when(lat + 1 < bands)
    def _():
        up_copy().start()

    @pl.when(lat > 0)
    def _():
        dn_copy().start()

    orders = [[*range(1, bits), 0], [*range(bits - 1, 0, -1), 0]]

    def weight_copies(m, phase):
        order = orders[m % 2]
        held = [me]
        for bit in order[:phase]:
            held = held + [flipped(h, bit) for h in held]
        to = flipped(me, order[phase])
        out = []
        for n, h in enumerate(held):
            at = (1 << phase) - 1 + n
            out.append(
                pltpu.make_async_remote_copy(
                    src_ref=shards[m] if n == 0 else gathered[m].at[h],
                    dst_ref=gathered[m].at[h],
                    send_sem=w_send.at[m, at],
                    recv_sem=w_recv.at[m, at],
                    device_id={"comp": to},
                    device_id_type=MESH,
                )
            )
        return out

    def weight_phase(phase):
        for m in range(4):
            if phase:
                for copy in weight_copies(m, phase - 1):
                    copy.wait_recv()
            if phase < bits:
                for copy in weight_copies(m, phase):
                    copy.start()

    weight_phase(0)
    loads = [pltpu.make_async_copy(shards[m], own_s.at[m], own_sem.at[m]) for m in range(4)]
    for copy in loads:
        copy.start()

    @pl.when(lat == 0)
    def _():
        up_s[...] = jnp.zeros_like(up_s)

    @pl.when(lat + 1 == bands)
    def _():
        dn_s[...] = jnp.zeros_like(dn_s)

    @pl.loop(0, blocks)
    def _(i):
        size = CB * rows
        whole = moved(x_ref[pl.ds(pl.multiple_of(i * size, size), size), :], ones_ref[...])
        for v in range(ways):
            x_s[v] = whole[:, v * LANES : (v + 1) * LANES]
        for half in range(CB // 8):
            base = pl.multiple_of(i * CB + half * 8, 8)
            speed = speeds(cour_ref[pl.ds(base, 8), 0:1], lon)
            for r in range(rows):
                sea = mask_ref[margin + r : margin + r + 1, :]
                first = half * (8 * rows) + r
                e = jnp.concatenate([x_s[v, pl.ds(first, 8, stride=rows), :] for v in range(ways)], axis=1)
                swept_s[r, pl.ds(base, 8), :] = lon_row(e * sea, sea, speed)

    stores = [pltpu.make_async_copy(own_s.at[m], gathered[m].at[me], own_sem.at[4 + m]) for m in range(4)]
    for m in range(4):
        loads[m].wait()
        stores[m].start()

    @pl.when(lat > 0)
    def _():
        up_copy().wait_recv()

    @pl.when(lat + 1 < bands)
    def _():
        dn_copy().wait_recv()

    if bits > 1:
        weight_phase(1)

    def point_copy(k, i):
        to = (me + k) % dests
        at = pl.ds(pl.multiple_of(i * CB, CB), CB)
        return pltpu.make_async_remote_copy(
            src_ref=send_s.at[to, at],
            dst_ref=pts_ref.at[me, at],
            send_sem=p_send.at[k - 1, i],
            recv_sem=p_recv.at[k - 1, i],
            device_id={"comp": to},
            device_id_type=MESH,
        )

    @pl.loop(0, blocks)
    def _(i):
        both = pl.ds(pl.multiple_of(i * CB, CB), CB)
        for k in range(2 * margin):
            src = up_s if k < margin else dn_s
            u_s[k] = jnp.dot(src[k % margin, both, :], ones_ref[...], preferred_element_type=jnp.float32)

        @pl.loop(0, CB // 8)
        def _(half):
            base = pl.multiple_of(i * CB + half * 8, 8)
            cour = cour_ref[pl.ds(base, 8), :]
            lon_speed = speeds(cour[:, 0:1], lon)
            c, a, pos = speeds(cour[:, 1:2], lon)

            def sea_row(r):
                return mask_ref[r : r + 1, :]

            def swept_row(r):
                if margin <= r < margin + rows:
                    return swept_s[r - margin, pl.ds(base, 8), :]
                return a_s[r]

            for k in range(2 * margin):
                r = k if k < margin else rows + k
                sea = sea_row(r)
                e = u_s[k, pl.ds(pl.multiple_of(half * 8, 8), 8), :] * sea
                a_s[r] = lon_row(e, sea, lon_speed)

            for substep in range(ADV):
                gone = 2 * substep
                row = swept_row
                if substep:
                    for r in range(gone, total - gone):
                        a_s[r] = lon_row(b_s[r], sea_row(r), lon_speed)
                    row = lambda r: a_s[r]
                cur, nxt, ahead = row(gone), row(gone + 1), row(gone + 2)
                d, dp, fl = nxt - cur, ahead - nxt, None
                for r in range(gone + 1, total - gone - 2):
                    cur, nxt, dm, d = nxt, ahead, d, dp
                    ahead = row(r + 2)
                    dp = ahead - nxt
                    now = c * jnp.where(pos, cur, nxt) + a * half_limited(jnp.where(pos, dm, dp), d)
                    if fl is not None:
                        value = sea_row(r) * (cur - (now - fl))
                        if substep == ADV - 1:
                            at = (r - margin) * lon
                            while at < (r - margin + 1) * lon:
                                to, lane = divmod(at, chunk)
                                n = min(chunk - lane, lon - at % lon)
                                band_ref[to, pl.ds(base, 8), lane : lane + n] = value[:, at % lon : at % lon + n]
                                at += n
                        else:
                            b_s[r] = value
                    fl = now

        for d in range(dests):
            value = band_ref[d, both, :] * STEPS + 0.5
            send_s[d, both, :] = value.astype(jnp.int32).astype(jnp.int16)
        for k in range(1, dests):
            point_copy(k, i).start()

    own_points = pltpu.make_async_copy(send_s.at[me], pts_ref.at[me], own_sem.at[8])
    own_points.start()
    for phase in range(2, bits + 1):
        weight_phase(phase)
    own_points.wait()
    for m in range(4):
        stores[m].wait()
        for phase in range(bits):
            for copy in weight_copies(m, phase):
                copy.wait_send()

    @pl.when(lat + 1 < bands)
    def _():
        up_copy().wait_send()

    @pl.when(lat > 0)
    def _():
        dn_copy().wait_send()

    @pl.loop(0, blocks)
    def _(i):
        for k in range(1, dests):
            point_copy(k, i).wait()


def advect(spectrum, top, end, mask_rows, cour, weights, dests, bands):
    comps, rows, lon = spectrum.shape
    chunk = rows * lon // dests
    margin = 2 * ADV
    total = rows + 2 * margin
    shard = weights[0].shape
    vmem = pl.BlockSpec(memory_space=pltpu.VMEM)
    hbm = pl.BlockSpec(memory_space=pl.ANY)
    copies = dests - 1
    dma = pltpu.SemaphoreType.DMA
    return pl.pallas_call(
        functools.partial(advect_kernel, rows, dests, bands),
        in_specs=[vmem] * 6 + [hbm] * 4,
        out_specs=[vmem] + [hbm] * 5,
        out_shape=[
            jax.ShapeDtypeStruct((dests, comps, chunk), jnp.float32),
            jax.ShapeDtypeStruct((dests, comps, chunk), jnp.int16),
        ]
        + [jax.ShapeDtypeStruct((dests, *shard), w.dtype) for w in weights],
        scratch_shapes=[
            pltpu.VMEM((lon // LANES, CB * rows, LANES), jnp.float32),
            pltpu.VMEM((rows, comps, lon), jnp.float32),
            pltpu.VMEM((total, 8, lon), jnp.float32),
            pltpu.VMEM((total, 8, lon), jnp.float32),
            pltpu.VMEM((2 * margin, CB, lon), jnp.float32),
            pltpu.VMEM((margin, comps, lon), jnp.bfloat16),
            pltpu.VMEM((margin, comps, lon), jnp.bfloat16),
            pltpu.VMEM((dests, comps, chunk), jnp.int16),
            pltpu.VMEM((4, *shard), jnp.bfloat16),
            dma((2,)),
            dma((2,)),
            dma((4, copies)),
            dma((4, copies)),
            dma((copies, comps // CB)),
            dma((copies, comps // CB)),
            dma((9,)),
        ],
        compiler_params=pltpu.CompilerParams(
            collective_id=0, has_side_effects=True, vmem_limit_bytes=60 * 1024 * 1024
        ),
        name="advect",
    )(spectrum.reshape(comps * rows, lon), top, end, mask_rows, cour, spreader(lon), *weights)


def finish_kernel(rows, band_ref, delta_ref, ones_ref, out_ref, f_s):
    dests, cb, chunk = band_ref.shape
    lon = out_ref.shape[1]
    for r in range(rows):
        at = 0
        while at < lon:
            d, lane = divmod(r * lon + at, chunk)
            n = min(chunk - lane, lon - at)
            v = band_ref[d, :, lane : lane + n] + delta_ref[d, :, lane : lane + n].astype(jnp.float32)
            for j in range(n // LANES):
                f_s[at // LANES + j, pl.ds(r, cb, stride=rows), :] = v[:, j * LANES : (j + 1) * LANES]
            at += n
    whole = jnp.concatenate([f_s[v] for v in range(lon // LANES)], axis=1)
    out_ref[...] = moved(whole, ones_ref[...])


def finish(band, delta, rows, lon):
    dests, comps, chunk = band.shape
    blk = pl.BlockSpec((dests, CB, chunk), lambda i: (0, i, 0))
    out = pl.pallas_call(
        functools.partial(finish_kernel, rows),
        grid=(pl.cdiv(comps, CB),),
        in_specs=[blk, blk, pl.BlockSpec((lon, lon), lambda i: (0, 0))],
        out_specs=pl.BlockSpec((CB * rows, lon), lambda i: (i, 0)),
        out_shape=jax.ShapeDtypeStruct((comps * rows, lon), jnp.float32),
        scratch_shapes=[pltpu.VMEM((lon // LANES, CB * rows, LANES), jnp.float32)],
        name="finish",
    )(band, delta, spreader(lon, back=True))
    return out.reshape(comps, rows, lon)


NT = (((1,), (1,)), ((), ()))


def ocean_kernel(prof_ref, pts_ref, east_ref, north_ref, live_ref, vort_ref, diff_ref, out_ref, p_s, s_s):
    layers, points = prof_ref.shape
    slots = pts_ref.shape[0]
    per = LOW // layers
    for k in range(points // LOW):
        p_s[k * layers : (k + 1) * layers, :] = prof_ref[:, k * LOW : (k + 1) * LOW]
    lane = lax.broadcasted_iota(jnp.int32, (LOW, LOW), 1)
    block = lane // layers

    def pick(index, count, product):
        low = jnp.broadcast_to(index % LOW, (LOW, LOW))
        high = jnp.broadcast_to(index // LOW, (LOW, LOW)) - block
        hot = jnp.where(low == lane, 1.0, 0.0).astype(jnp.bfloat16)
        acc = jnp.zeros((LOW, LOW), jnp.float32)
        for m in range(-(-count // per)):
            acc = acc + jnp.where(high == m * per, product(hot, m), 0.0)
        return sum(acc[:, i * layers : (i + 1) * layers] for i in range(per))

    def from_points(hot, m):
        return lax.dot_general(hot, p_s[m * LOW : (m + 1) * LOW, :], NT, preferred_element_type=jnp.float32)

    s_s[...] = jnp.zeros_like(s_s)
    for j in range(slots // LOW):
        s = pick(pts_ref[j * LOW : (j + 1) * LOW, :], points // LOW, from_points)
        s_s[:, j * layers : (j + 1) * layers] = s.astype(jnp.bfloat16)

    def from_slots(hot, m):
        return jnp.dot(hot, s_s[:, m * LOW : (m + 1) * LOW], preferred_element_type=jnp.float32)

    for j in range(slots // LOW):
        rows = slice(j * LOW, (j + 1) * LOW)
        gap = pick(east_ref[rows, :], slots // LOW, from_slots) - pick(north_ref[rows, :], slots // LOW, from_slots)
        gap = gap.T
        s = s_s[:, j * layers : (j + 1) * layers].astype(jnp.float32).T
        upper = jnp.concatenate([s[:1], s[:-1]], axis=0)
        lower = jnp.concatenate([s[1:], jnp.zeros_like(s[:1])], axis=0)
        out_ref[:, rows] = live_ref[:, rows] * (
            vort_ref[:, rows] * gap + diff_ref[:, rows] * (upper - 2.0 * s + lower)
        )


def ocean(profile, pts, count, nbr, vort, diff):
    layers, points = profile.shape
    slots = pts.shape[0]
    per = LOW // layers
    lanes = -(-(slots // LOW) // per) * LOW
    live = (jnp.arange(slots, dtype=jnp.int32) < count).astype(jnp.float32)[None]
    return pl.pallas_call(
        ocean_kernel,
        out_shape=jax.ShapeDtypeStruct((layers, slots), jnp.float32),
        scratch_shapes=[
            pltpu.VMEM((points // LOW * layers, LOW), jnp.bfloat16),
            pltpu.VMEM((LOW, lanes), jnp.bfloat16),
        ],
        name="ocean",
    )(profile, pts[:, None], nbr[0][:, None], nbr[1][:, None], live, vort, diff)


def contract(weights, operand):
    return lax.dot_general(
        weights, operand, (((0,), (0,)), ((), ())), preferred_element_type=jnp.float32
    )


def on_device(
    spectrum,
    mask,
    courant,
    proj_a,
    proj_b,
    proj_c,
    proj_d,
    stokes_kernel,
    tile_points,
    tile_counts,
    tile_nbr,
    vorticity,
    diffusivity,
):
    comps, rows, lon = spectrum.shape
    margin = 2 * ADV
    bands, dests = lax.axis_size("lat"), lax.axis_size("comp")
    band_index = lax.axis_index("lat")
    sea = jnp.pad(mask.astype(jnp.float32), ((margin, margin), (0, 0)))
    ways = lon // LANES
    sea = sea.reshape(-1, LANES, ways).transpose(0, 2, 1).reshape(-1, lon)
    mask_rows = lax.dynamic_slice_in_dim(sea, band_index * rows, rows + 2 * margin, 0)
    padded = pl.cdiv(comps, CB) * CB
    spread = ((0, padded - comps), (0, 0), (0, 0))
    top = spectrum[:, :margin].astype(jnp.bfloat16).transpose(1, 0, 2)
    end = spectrum[:, rows - margin :].astype(jnp.bfloat16).transpose(1, 0, 2)
    weights = (proj_a, proj_b, proj_c, proj_d)
    cour = courant.T
    start = spectrum
    if padded != comps:
        start = jnp.pad(spectrum, spread)
        cour = jnp.pad(cour, spread[:2])
        top, end = (jnp.pad(part, (spread[1], spread[0], spread[2])) for part in (top, end))
    band, points, *weights = advect(start, top, end, mask_rows, cour, weights, dests, bands)
    band, points = band[:, :comps], points[:, :comps]
    weights = [w.reshape(dests * comps, -1) for w in weights]
    chunk = points.shape[2]
    points = points.reshape(dests * comps, chunk)
    own = points.astype(jnp.float32) * (1.0 / STEPS)
    points = own.astype(jnp.bfloat16)
    product = (contract(weights[0], points) * contract(weights[1], points)).astype(jnp.bfloat16)
    delta = time_step * (contract(weights[2], product) - own * contract(weights[3], product))
    profile = lax.dot_general(
        stokes_kernel, own + delta, (((0,), (0,)), ((), ())), precision=lax.Precision.HIGHEST
    ).astype(jnp.bfloat16)
    group = lax.all_gather(profile, "comp", axis=1, tiled=True)
    back = lax.all_to_all(
        delta.astype(jnp.bfloat16).reshape(dests, comps, chunk), "comp", split_axis=0, concat_axis=0
    )
    where = tile_points[0, 0]
    cell = where % lon
    where = where - cell + cell % ways * LANES + cell // ways
    force = ocean(group, where, tile_counts[0, 0], tile_nbr[0, 0], vorticity[0, 0], diffusivity[0, 0])
    return finish(band, back, rows, lon), force[None, None]


def solution(mesh):
    return jax.shard_map(
        on_device,
        mesh=mesh,
        in_specs=(
            P("comp", "lat", None),
            P(),
            P(None, "comp"),
            P("comp", None),
            P("comp", None),
            P("comp", None),
            P("comp", None),
            P(),
            P("lat", "comp", None),
            P("lat", "comp"),
            P("lat", "comp", None, None),
            P("lat", "comp", None, None),
            P("lat", "comp", None, None),
        ),
        out_specs=(P("comp", "lat", None), P("lat", "comp", None, None)),
        check_vma=False,
    )
```

time: 276 us -> 188 us (0.68)
  blocking collectives: 22.1 us -> 0 us
  matrix products: 42.1 us -> 22.7 us
  Pallas kernels: 115 us -> 101 us
  waiting for transfers between devices: 33.4 us -> 21.4 us
  starting transfers between devices: 14.8 us -> 3.96 us
  local copies, waits for them, and re-layouts: 19 us -> 13.8 us
  other arithmetic: 13.6 us -> 9.29 us
    all_to_all x1 -> x0, blocking collectives: 22.1 us -> none  [on_device(): lax.all_to_all(piece.astype(jnp.float16), 'comp', split_axis=0, concat_ax...]
    dot_general x4, matrix products: 32.9 us -> 16.7 us  [contract(): lax.dot_general(weights, operand, (((0,), (0,)), ((), ())), preferred_ele...]
    pallas_call x2 -> x1, Pallas kernels: 95.7 us -> 80.5 us  [advect(): pl.pallas_call(functools.partial(advect_kernel, rows, dests, bands), in_s...]
    ppermute x2 -> x0, waiting for transfers between devices: 14 us -> none  [the longest x1 9.7 us: on_device(): halo_up = lax.ppermute(edge(spectrum[:, rows - margin:]), 'lat', up)]
    convert_element_type x2 -> x0, local copies, waits for them, and re-layouts: 9.45 us -> none  [the longest x1 6.91 us: on_device(): own = points.astype(jnp.float32)]
    convert_element_type x3 -> x1, other arithmetic: 7.9 us -> 1.46 us  [spreader(): return (x == at % LANES * ways + at // LANES).astype(jnp.bfloat16)]
    ppermute x2 -> x0, starting transfers between devices: 6.29 us -> none  [the longest x1 4.99 us: on_device(): halo_up = lax.ppermute(edge(spectrum[:, rows - margin:]), 'lat', up)]
    unnamed x23 -> x24, local copies, waits for them, and re-layouts: 1.84 us -> 7.67 us
  transfers between devices with their start and end apart: 9 -> 2, of which waited for: 3 -> 1; matrix products, arithmetic and copies ran while one was open for 22% -> 8% of each run, Pallas kernels for 39% -> 6%
where the time goes in v2:
time: 188 us; the launch traced here: 187 us
  Pallas kernels  101 us (54%)
  matrix products  22.7 us (12%)
  waiting for transfers between devices  21.4 us (11%)
  between operations  14.9 us (8%)
  local copies, waits for them, and re-layouts  13.8 us (7%)
  other arithmetic  9.29 us (5%)
  starting transfers between devices  3.96 us (2%)
    pallas_call x1, Pallas kernels, advect(): pl.pallas_call(functools.partial(advect_kernel, rows, dests, bands), in_s...  80.5 us
    all_gather x1, waiting for transfers between devices, on_device(): group = lax.all_gather(profile, 'comp', axis=1, tiled=True)  21.4 us
    dot_general x4, matrix products, contract(): lax.dot_general(weights, operand, (((0,), (0,)), ((), ())), preferred_ele...  16.7 us
    pallas_call x1, Pallas kernels, ocean(): pl.pallas_call(ocean_kernel, out_shape=jax.ShapeDtypeStruct((layers, slot...  10.6 us
    pallas_call x1, Pallas kernels, finish(): pl.pallas_call(functools.partial(finish_kernel, rows), grid=(pl.cdiv(comp...  10.2 us
    unnamed x24, local copies, waits for them, and re-layouts  7.67 us
    dot_general x1, matrix products, on_device(): lax.dot_general(stokes_kernel, own + delta, (((0,), (0,)), ((), ())), pre...  6.07 us
  transfers between devices with their start and end apart: 2, of which 1 were waited for; matrix products, arithmetic and copies ran while one was open for 8% of the time, Pallas kernels for 6%

profile of v2, /device:TPU:0, one launch (start us, length us, event | category | flops | bytes accessed | tf_op | source)
XLA Modules:
  0.0 187.5 jit_solution(8672682715072701801)
XLA Ops:
  7.2 0.0 copy-start
  7.2 1.0 convert_element_type.46
  8.2 0.1 copy.38
  8.3 0.1 pad.4.clone
  8.4 0.1 copy.30
  8.6 0.0 copy-start.6
  8.6 4.9 %copy.42 = bf16[144,16,512]{2,0,1:T(8,128)(2,1)S(1)} copy(f32[144,16,512]{2,1,0:T(8,128)} %param.13) | data formatting | bytes 7077888 | tf_op args[0]
  13.5 1.1 slice_bitcast_fusion
  14.6 0.0 copy-done.6
  14.6 0.7 copy.31
  15.3 0.6 constant_dynamic-slice_fusion.mask_ref
  15.9 1.5 fusion.12
  17.4 80.5 %advect.1 = (f32[8,144,1024]{2,1,0:T(8,128)}, s16[8,144,1024]{2,1,0:T(8,128)(2,1)}, bf16[8,144,1152]{2,1,0:T(8,128)(2,1)}, bf16[8,144,1152]{2,1,0:T(8,128)(2,1)}...) custom-call(f32[2304,512]{1,0:T(8,128)} %bitcast.46, bf16[4,144,512]{2,1,0:T(8,128)(2,1)} %get-tuple-element.17.top_ref, ...), custom_call_target="tpu_custom_call" | custom-call | tf_op jit(solution)/shard_map/advect/pallas_call | solution.py:302
  97.9 0.0 copy-start.3
  97.9 0.0 copy-start.9
  97.9 2.7 %convert_multiply_fusion = f32[8,144,1024]{2,1,0:T(8,128)S(1)} fusion(s16[8,144,1024]{2,1,0:T(8,128)(2,1)} %get-tuple-element.11), kind=kLoop, calls=%fused_computation.6 | loop fusion | flops 2359296 | bytes 7077888 | tf_op jit(solution)/shard_map/mul | solution.py:473
  100.6 0.0 copy-done.3
  100.6 0.5 copy-done.9
  101.1 0.0 copy-start.8
  101.1 3.4 %fusion.2 = f32[1152,1024,1]{1,0,2:T(8,128)S(1)} fusion(bf16[8,144,1152]{2,1,0:T(8,128)(2,1)S(1)} %copy-done.9, s16[8,144,1024]{2,1,0:T(8,128)(2,1)S(1)} %copy-done.3), kind=kOutput, calls=%fused_computation.16 | convolution fusion | flops 2721447936 | bytes 9732096 | tf_op jit(solution)/shard_map/dot_general | solution.py:429
  104.5 0.0 copy-done.8
  104.5 0.0 copy-start.7
  104.5 3.6 %fusion = bf16[1152,1024]{1,0:T(8,128)(2,1)S(1)} fusion(f32[1152,1024,1]{1,0,2:T(8,128)S(1)} %fusion.2, bf16[8,144,1152]{2,1,0:T(8,128)(2,1)S(1)} %copy-done.8, s16[8,144,1024]{2,1,0:T(8,128)(2,1)S(1)} %copy-done.3), kind=kOutput, calls=%fused_computation.3 | convolution fusion | flops 2723807232 | bytes 12091392 | tf_op jit(solution)/shard_map/dot_general | solution.py:429
  108.1 0.0 copy-done.7
  108.2 0.0 copy-start.2
  108.2 3.3 %fusion.24 = f32[1152,1024]{1,0:T(8,128)S(1)} fusion(bf16[1152,1152]{1,0:T(8,128)(2,1)S(1)} %bitcast.57, bf16[1152,1024]{1,0:T(8,128)(2,1)S(1)} %fusion), kind=kOutput, calls=%fused_computation.53 | convolution fusion | flops 2717908992 | bytes 9732096 | tf_op jit(solution)/shard_map/dot_general | solution.py:429
  111.5 0.0 copy-done.2
  111.5 6.3 %bitcast_add_fusion = (f32[1152,1024]{1,0:T(8,128)}, bf16[1152,1024]{1,0:T(8,128)(2,1)}) fusion(f32[8,144,1024]{2,1,0:T(8,128)S(1)} %convert_multiply_fusion, f32[1152,1024]{1,0:T(8,128)S(1)} %fusion.24, f32[1152,1024]{1,0:T(8,128)S(1)} %bitcast.45, bf16[1152,1152]{1,0:T(8,128)(2,1)S(1)} %bitcast.47, bf16[1152,1024]{1,0:T(8,128)(2,1)S(1)} %fusion), kind=kOutput, calls=%fused_computation.1 | convolution fusion | flops 2723807232 | bytes 26247168 | tf_op jit(solution)/shard_map/dot_general | solution.py:429
  117.8 3.7 %all-to-all-start = ((bf16[8,144,1024]{2,1,0:T(8,128)(2,1)}), bf16[8,144,1024]{2,1,0:T(8,128)(2,1)S(1)}, u32[]{:S(2)}, u32[]{:S(2)}) async-start(bf16[8,144,1024]{2,1,0:T(8,128)(2,1)} %bitcast.11), calls=%async_computation | async-start | bytes 4718592 | tf_op jit(solution)/shard_map/all_to_all | solution.py:481
  121.5 0.0 copy-start.4
  121.5 0.3 all-gather.2.cloned.1.call-start
  121.8 0.0 copy-done
  121.8 0.0 copy-start.5
  121.8 6.1 %fusion.4 = bf16[64,1024]{1,0:T(8,128)(2,1)} fusion(f32[1152,1024]{1,0:T(8,128)} %get-tuple-element.14, f32[1152,64]{0,1:T(8,128)S(1)} %copy-done), kind=kOutput, calls=%fused_computation.19 | convolution fusion | flops 906035200 | bytes 5144576 | tf_op jit(solution)/shard_map/dot_general | solution.py:477
  127.9 0.0 all-gather.2.cloned.1.call-update
  127.9 0.0 copy-done.4
  128.0 1.4 copy.36.east_ref
  129.4 1.3 copy.37.north_ref
  130.7 0.0 copy-done.5
  130.7 1.3 copy.35
  132.7 0.6 compare_convert_fusion.live_ref
  133.3 3.6 %fusion.8.pts_ref = s32[2048,1]{1,0:T(8,128)} fusion(s32[2048,1]{1,0:T(8,128)} %copy.35), kind=kLoop, calls=%fused_computation.23 | loop fusion | flops 69632 | bytes 16384 | tf_op jit(solution)/shard_map/add | solution.py:486
  136.9 21.4 %all-gather.2.cloned.1.call-done.prof_ref = bf16[64,8192]{1,0:T(8,128)(2,1)} async-done(((bf16[64,1024]{1,0:T(8,128)(2,1)}), bf16[64,8192]{1,0:T(8,128)(2,1)}) %all-gather.2.cloned.1.call-update) | async-done | bytes 1048592 | tf_op jit(solution)/shard_map/all_gather | solution.py:480
  158.3 10.6 %ocean.1 = f32[64,2048]{1,0:T(8,128)} custom-call(bf16[64,8192]{1,0:T(8,128)(2,1)} %all-gather.2.cloned.1.call-done.prof_ref, s32[2048,1]{1,0:T(8,128)} %fusion.8.pts_ref, s32[2048,1]{1,0:T(8,128)} %copy.36.east_ref, s32[2048,1]{1,0:T(8,128)} %copy.37.north_ref, f32[1,2048]{1,0:T(1,128)} %compare_convert_fusion.live_ref, f32[64,2048]{1,0:T(8,128)} %bitcast.51, ...), custom_call_target="tpu_custom_call" | custom-call | tf_op jit(solution)/shard_map/ocean/pallas_call | solution.py:417
  168.9 0.0 all-to-all-done.delta_ref
  169.0 0.0 copy-start.1
  169.0 1.4 copy-done.1
  170.4 10.2 %finish.1 = f32[2304,512]{1,0:T(8,128)} custom-call(f32[8,144,1024]{2,1,0:T(8,128)} %get-tuple-element.8.band_ref, bf16[8,144,1024]{2,1,0:T(8,128)(2,1)} %copy-done.1, bf16[512,512]{1,0:T(8,128)(2,1)} %get-tuple-element.20.ones_ref), custom_call_target="tpu_custom_call" | custom-call | tf_op jit(solution)/shard_map/finish/pallas_call | solution.py:355
  (5 shorter events, 0.0 us)
Async XLA Ops:
  7.2 114.6 %copy-start = (f32[1152,64]{0,1:T(8,128)S(1)}, f32[1152,64]{0,1:T(8,128)}, u32[]{:S(2)}) copy-start(f32[1152,64]{0,1:T(8,128)} %param.20) | copy-start | bytes 884740
  8.6 6.0 %copy-start.6 = (f32[2,144]{1,0:T(2,128)S(1)}, f32[2,144]{1,0:T(2,128)}, u32[]{:S(2)}) copy-start(f32[2,144]{1,0:T(2,128)} %param.15) | copy-start | bytes 3460
  97.9 2.7 %copy-start.3 = (s16[8,144,1024]{2,1,0:T(8,128)(2,1)S(1)}, s16[8,144,1024]{2,1,0:T(8,128)(2,1)}, u32[]{:S(2)}) copy-start(s16[8,144,1024]{2,1,0:T(8,128)(2,1)} %get-tuple-element.11) | copy-start | bytes 7077892
  97.9 3.2 %copy-start.9 = (bf16[8,144,1152]{2,1,0:T(8,128)(2,1)S(1)}, bf16[8,144,1152]{2,1,0:T(8,128)(2,1)}, u32[]{:S(2)}) copy-start(bf16[8,144,1152]{2,1,0:T(8,128)(2,1)} %get-tuple-element.10) | copy-start | bytes 7962628
  101.1 3.4 %copy-start.8 = (bf16[8,144,1152]{2,1,0:T(8,128)(2,1)S(1)}, bf16[8,144,1152]{2,1,0:T(8,128)(2,1)}, u32[]{:S(2)}) copy-start(bf16[8,144,1152]{2,1,0:T(8,128)(2,1)} %get-tuple-element.12) | copy-start | bytes 7962628
  104.5 3.7 %copy-start.7 = (bf16[8,144,1152]{2,1,0:T(8,128)(2,1)S(1)}, bf16[8,144,1152]{2,1,0:T(8,128)(2,1)}, u32[]{:S(2)}) copy-start(bf16[8,144,1152]{2,1,0:T(8,128)(2,1)} %get-tuple-element.9) | copy-start | bytes 7962628
  108.2 3.4 %copy-start.2 = (bf16[8,144,1152]{2,1,0:T(8,128)(2,1)S(1)}, bf16[8,144,1152]{2,1,0:T(8,128)(2,1)}, u32[]{:S(2)}) copy-start(bf16[8,144,1152]{2,1,0:T(8,128)(2,1)} %get-tuple-element.13) | copy-start | bytes 7962628
  117.8 51.1 %all-to-all-start = ((bf16[8,144,1024]{2,1,0:T(8,128)(2,1)}), bf16[8,144,1024]{2,1,0:T(8,128)(2,1)S(1)}, u32[]{:S(2)}, u32[]{:S(2)}) async-start(bf16[8,144,1024]{2,1,0:T(8,128)(2,1)} %bitcast.11), calls=%async_computation | async-start | bytes 4718592 | tf_op jit(solution)/shard_map/all_to_all | solution.py:481
  121.5 6.4 %copy-start.4 = (s32[1,1,2,2048]{3,2,1,0:T(2,128)S(1)}, s32[1,1,2,2048]{3,2,1,0:T(2,128)}, u32[]{:S(2)}) copy-start(s32[1,1,2,2048]{3,2,1,0:T(2,128)} %param.23) | copy-start | bytes 49156
  121.5 36.8 %all-gather.2.cloned.1.call-start = ((), (), s32[]{:S(2)}) async-start(), calls=%async_computation.1 | async-start | bytes 1179648 | tf_op jit(solution)/shard_map/all_gather | solution.py:480
  121.8 8.9 %copy-start.5 = (s32[1,1,2048]{2,1,0:T(1,128)S(1)}, s32[1,1,2048]{2,1,0:T(1,128)}, u32[]{:S(2)}) copy-start(s32[1,1,2048]{2,1,0:T(1,128)} %param.21) | copy-start | bytes 24580
  169.0 1.4 copy-start.1
Sparse Core Ops, SparseCore 0:
  128.0 30.2 all-gather.1

commit v3 on v2

--- a/solution.py
+++ b/solution.py
@@ -64,9 +64,9 @@
 
 
 def advect_kernel(
-    rows, dests, bands, x_ref, top_ref, end_ref, mask_ref, cour_ref, ones_ref, wa, wb, wc, wd,
+    rows, dests, bands, x_ref, top_ref, end_ref, land_ref, cour_ref, ones_ref, wa, wb, wc, wd,
     band_ref, pts_ref, ga, gb, gc, gd,
-    x_s, swept_s, a_s, b_s, u_s, up_s, dn_s, send_s, own_s,
+    mask_ref, x_s, swept_s, a_s, b_s, u_s, up_s, dn_s, send_s, own_s,
     halo_send, halo_recv, w_send, w_recv, p_send, p_recv, own_sem,
 ):
     lon = ones_ref.shape[0]
@@ -160,6 +160,8 @@
     def _():
         dn_s[...] = jnp.zeros_like(dn_s)
 
+    mask_ref[...] = jnp.dot(land_ref[...].astype(jnp.bfloat16), ones_ref[...], preferred_element_type=jnp.float32)
+
     @pl.loop(0, blocks)
     def _(i):
         size = CB * rows
@@ -180,16 +182,16 @@
         loads[m].wait()
         stores[m].start()
 
-    @pl.when(lat > 0)
-    def _():
-        up_copy().wait_recv()
-
-    @pl.when(lat + 1 < bands)
-    def _():
-        dn_copy().wait_recv()
-
     if bits > 1:
         weight_phase(1)
+
+    @pl.when(lat > 0)
+    def _():
+        up_copy().wait_recv()
+
+    @pl.when(lat + 1 < bands)
+    def _():
+        dn_copy().wait_recv()
 
     def point_copy(k, i):
         to = (me + k) % dests
@@ -309,6 +311,7 @@
         ]
         + [jax.ShapeDtypeStruct((dests, *shard), w.dtype) for w in weights],
         scratch_shapes=[
+            pltpu.VMEM((total, lon), jnp.float32),
             pltpu.VMEM((lon // LANES, CB * rows, LANES), jnp.float32),
             pltpu.VMEM((rows, comps, lon), jnp.float32),
             pltpu.VMEM((total, 8, lon), jnp.float32),
@@ -364,65 +367,85 @@
     return out.reshape(comps, rows, lon)
 
 
-NT = (((1,), (1,)), ((), ()))
-
-
-def ocean_kernel(prof_ref, pts_ref, east_ref, north_ref, live_ref, vort_ref, diff_ref, out_ref, p_s, s_s):
-    layers, points = prof_ref.shape
-    slots = pts_ref.shape[0]
+def ocean_kernel(lon, prof_ref, pts_ref, nbr_ref, count_ref, vort_ref, diff_ref, out_ref, g_s, p_s, s_s, send, recv):
+    dests, layers, chunk = g_s.shape
+    slots = pts_ref.shape[1]
     per = LOW // layers
-    for k in range(points // LOW):
-        p_s[k * layers : (k + 1) * layers, :] = prof_ref[:, k * LOW : (k + 1) * LOW]
-    lane = lax.broadcasted_iota(jnp.int32, (LOW, LOW), 1)
-    block = lane // layers
-
-    def pick(index, count, product):
+    ways = lon // LANES
+    me = lax.axis_index("comp")
+    barrier = pltpu.get_barrier_semaphore()
+    for k in range(1, dests):
+        pl.semaphore_signal(barrier, inc=1, device_id={"comp": (me + k) % dests}, device_id_type=MESH)
+    pl.semaphore_wait(barrier, dests - 1)
+    copies = [
+        pltpu.make_async_remote_copy(
+            src_ref=prof_ref,
+            dst_ref=g_s.at[me],
+            send_sem=send.at[k - 1],
+            recv_sem=recv.at[k - 1],
+            device_id={"comp": (me + k) % dests},
+            device_id_type=MESH,
+        )
+        for k in range(1, dests)
+    ]
+    for copy in copies:
+        copy.start()
+    g_s[me] = prof_ref[...]
+    s_s[...] = jnp.zeros_like(s_s)
+    row = lax.broadcasted_iota(jnp.int32, (LOW, LOW), 0)
+    block = row // layers
+
+    def pick(index, count, source):
         low = jnp.broadcast_to(index % LOW, (LOW, LOW))
         high = jnp.broadcast_to(index // LOW, (LOW, LOW)) - block
-        hot = jnp.where(low == lane, 1.0, 0.0).astype(jnp.bfloat16)
+        hot = jnp.where(low == row, 1.0, 0.0).astype(jnp.bfloat16)
         acc = jnp.zeros((LOW, LOW), jnp.float32)
         for m in range(-(-count // per)):
-            acc = acc + jnp.where(high == m * per, product(hot, m), 0.0)
-        return sum(acc[:, i * layers : (i + 1) * layers] for i in range(per))
-
-    def from_points(hot, m):
-        return lax.dot_general(hot, p_s[m * LOW : (m + 1) * LOW, :], NT, preferred_element_type=jnp.float32)
-
-    s_s[...] = jnp.zeros_like(s_s)
+            product = jnp.dot(source[m * LOW : (m + 1) * LOW, :], hot, preferred_element_type=jnp.float32)
+            acc = acc + jnp.where(high == m * per, product, 0.0)
+        return sum(acc[i * layers : (i + 1) * layers] for i in range(per))
+
+    for copy in copies:
+        copy.wait()
+    for d in range(dests):
+        for j in range(chunk // LOW):
+            k = d * (chunk // LOW) + j
+            p_s[k * layers : (k + 1) * layers, :] = g_s[d, :, j * LOW : (j + 1) * LOW]
     for j in range(slots // LOW):
-        s = pick(pts_ref[j * LOW : (j + 1) * LOW, :], points // LOW, from_points)
-        s_s[:, j * layers : (j + 1) * layers] = s.astype(jnp.bfloat16)
-
-    def from_slots(hot, m):
-        return jnp.dot(hot, s_s[:, m * LOW : (m + 1) * LOW], preferred_element_type=jnp.float32)
-
+        index = pts_ref[:, j * LOW : (j + 1) * LOW]
+        cell = index % lon
+        index = index - cell + cell % ways * LANES + cell // ways
+        s = pick(index, dests * chunk // LOW, p_s)
+        s_s[j * layers : (j + 1) * layers, :] = s.astype(jnp.bfloat16)
+    lane = lax.broadcasted_iota(jnp.int32, (1, LOW), 1)
     for j in range(slots // LOW):
-        rows = slice(j * LOW, (j + 1) * LOW)
-        gap = pick(east_ref[rows, :], slots // LOW, from_slots) - pick(north_ref[rows, :], slots // LOW, from_slots)
-        gap = gap.T
-        s = s_s[:, j * layers : (j + 1) * layers].astype(jnp.float32).T
+        part = slice(j * LOW, (j + 1) * LOW)
+        gap = pick(nbr_ref[0:1, part], slots // LOW, s_s) - pick(nbr_ref[1:2, part], slots // LOW, s_s)
+        s = s_s[j * layers : (j + 1) * layers, :].astype(jnp.float32)
         upper = jnp.concatenate([s[:1], s[:-1]], axis=0)
         lower = jnp.concatenate([s[1:], jnp.zeros_like(s[:1])], axis=0)
-        out_ref[:, rows] = live_ref[:, rows] * (
-            vort_ref[:, rows] * gap + diff_ref[:, rows] * (upper - 2.0 * s + lower)
-        )
-
-
-def ocean(profile, pts, count, nbr, vort, diff):
-    layers, points = profile.shape
-    slots = pts.shape[0]
+        live = jnp.where(lane + j * LOW < count_ref[...], 1.0, 0.0)
+        out_ref[:, part] = live * (vort_ref[:, part] * gap + diff_ref[:, part] * (upper - 2.0 * s + lower))
+
+
+def ocean(profile, pts, nbr, count, vort, diff, dests, lon):
+    layers, chunk = profile.shape
+    slots = pts.shape[1]
     per = LOW // layers
-    lanes = -(-(slots // LOW) // per) * LOW
-    live = (jnp.arange(slots, dtype=jnp.int32) < count).astype(jnp.float32)[None]
+    depth = -(-(slots // LOW) // per) * LOW
     return pl.pallas_call(
-        ocean_kernel,
+        functools.partial(ocean_kernel, lon),
         out_shape=jax.ShapeDtypeStruct((layers, slots), jnp.float32),
         scratch_shapes=[
-            pltpu.VMEM((points // LOW * layers, LOW), jnp.bfloat16),
-            pltpu.VMEM((LOW, lanes), jnp.bfloat16),
+            pltpu.VMEM((dests, layers, chunk), profile.dtype),
+            pltpu.VMEM((dests * chunk // LOW * layers, LOW), jnp.bfloat16),
+            pltpu.VMEM((depth, LOW), jnp.bfloat16),
+            pltpu.SemaphoreType.DMA((dests - 1,)),
+            pltpu.SemaphoreType.DMA((dests - 1,)),
         ],
+        compiler_params=pltpu.CompilerParams(collective_id=1, has_side_effects=True),
         name="ocean",
-    )(profile, pts[:, None], nbr[0][:, None], nbr[1][:, None], live, vort, diff)
+    )(profile, pts, nbr, count, vort, diff)
 
 
 def contract(weights, operand):
@@ -451,13 +474,11 @@
     bands, dests = lax.axis_size("lat"), lax.axis_size("comp")
     band_index = lax.axis_index("lat")
     sea = jnp.pad(mask.astype(jnp.float32), ((margin, margin), (0, 0)))
-    ways = lon // LANES
-    sea = sea.reshape(-1, LANES, ways).transpose(0, 2, 1).reshape(-1, lon)
     mask_rows = lax.dynamic_slice_in_dim(sea, band_index * rows, rows + 2 * margin, 0)
     padded = pl.cdiv(comps, CB) * CB
     spread = ((0, padded - comps), (0, 0), (0, 0))
-    top = spectrum[:, :margin].astype(jnp.bfloat16).transpose(1, 0, 2)
-    end = spectrum[:, rows - margin :].astype(jnp.bfloat16).transpose(1, 0, 2)
+    top, end = lax.optimization_barrier((spectrum[:, :margin], spectrum[:, rows - margin :]))
+    top, end = (part.astype(jnp.bfloat16).transpose(1, 0, 2) for part in (top, end))
     weights = (proj_a, proj_b, proj_c, proj_d)
     cour = courant.T
     start = spectrum
@@ -477,14 +498,12 @@
     profile = lax.dot_general(
         stokes_kernel, own + delta, (((0,), (0,)), ((), ())), precision=lax.Precision.HIGHEST
     ).astype(jnp.bfloat16)
-    group = lax.all_gather(profile, "comp", axis=1, tiled=True)
     back = lax.all_to_all(
         delta.astype(jnp.bfloat16).reshape(dests, comps, chunk), "comp", split_axis=0, concat_axis=0
     )
-    where = tile_points[0, 0]
-    cell = where % lon
-    where = where - cell + cell % ways * LANES + cell // ways
-    force = ocean(group, where, tile_counts[0, 0], tile_nbr[0, 0], vorticity[0, 0], diffusivity[0, 0])
+    force = ocean(
+        profile, tile_points[0], tile_nbr[0, 0], tile_counts, vorticity[0, 0], diffusivity[0, 0], dests, lon
+    )
     return finish(band, back, rows, lon), force[None, None]
 
 

time: 188 us -> 170 us (0.904)
  Pallas kernels: 101 us -> 127 us
  waiting for transfers between devices: 21.4 us -> 0.01 us
  between operations: 14.9 us -> 1.47 us
  local copies, waits for them, and re-layouts: 13.8 us -> 8.93 us
  other arithmetic: 9.29 us -> 5.11 us
    pallas_call x1, Pallas kernels: 10.6 us -> 36.2 us  [ocean(): pl.pallas_call(functools.partial(ocean_kernel, lon), out_shape=jax.ShapeD...]
    all_gather x1 -> x0, waiting for transfers between devices: 21.4 us -> none  [on_device(): group = lax.all_gather(profile, 'comp', axis=1, tiled=True)]
    unnamed x24 -> x20, local copies, waits for them, and re-layouts: 7.67 us -> 3.46 us
    add x1 -> x0, other arithmetic: 3.58 us -> none  [on_device(): where = where - cell + cell % ways * LANES + cell // ways]
    slice x0 -> x1, local copies, waits for them, and re-layouts: none -> 2.97 us  [on_device(): spectrum[:, rows - margin:]]
    another operation x3 -> x0, local copies, waits for them, and re-layouts: 2.78 us -> none  [the longest x1 1.43 us: ocean(): nbr[0][:, None]]
  transfers between devices with their start and end apart: 2 -> 1, of which waited for: 1 -> 0; matrix products, arithmetic and copies ran while one was open for 8% -> 4% of each run, Pallas kernels for 6% -> 21%
where the time goes in v3:
time: 170 us; the launch traced here: 169 us
  Pallas kernels  127 us (75%)
  matrix products  22.9 us (13%)
  local copies, waits for them, and re-layouts  8.93 us (5%)
  other arithmetic  5.11 us (3%)
  starting transfers between devices  3.64 us (2%)
    pallas_call x1, Pallas kernels, advect(): pl.pallas_call(functools.partial(advect_kernel, rows, dests, bands), in_s...  80.1 us
    pallas_call x1, Pallas kernels, ocean(): pl.pallas_call(functools.partial(ocean_kernel, lon), out_shape=jax.ShapeD...  36.2 us
    dot_general x4, matrix products, contract(): lax.dot_general(weights, operand, (((0,), (0,)), ((), ())), preferred_ele...  16.8 us
    pallas_call x1, Pallas kernels, finish(): pl.pallas_call(functools.partial(finish_kernel, rows), grid=(pl.cdiv(comp...  10.3 us
    dot_general x1, matrix products, on_device(): lax.dot_general(stokes_kernel, own + delta, (((0,), (0,)), ((), ())), pre...  6.06 us
    all_to_all x1, starting transfers between devices, on_device(): lax.all_to_all(delta.astype(jnp.bfloat16).reshape(dests, comps, chunk), '...  3.64 us
    unnamed x20, local copies, waits for them, and re-layouts  3.46 us
  transfers between devices with their start and end apart: 1, of which 0 were waited for; matrix products, arithmetic and copies ran while one was open for 4% of the time, Pallas kernels for 21%

profile of v3, /device:TPU:0, one launch (start us, length us, event | category | flops | bytes accessed | tf_op | source)
XLA Modules:
  0.0 168.6 jit_solution(5934400444637862223)
XLA Ops:
  0.6 0.0 copy-start
  0.6 0.0 copy-start.5
  0.7 1.0 convert_element_type.41
  1.7 3.0 %fusion.15 = (bf16[144,4,512]{2,1,0:T(4,128)(2,1)S(1)}, bf16[144,4,512]{2,1,0:T(4,128)(2,1)S(1)}) fusion(f32[144,16,512]{2,1,0:T(8,128)} %param.13), kind=kLoop, calls=%fused_computation.30 | loop fusion | bytes 2359296 | tf_op jit(solution)/shard_map/slice | solution.py:480
  4.6 0.9 copy.18
  5.5 1.0 copy.19
  6.5 0.0 copy-done.5
  6.5 0.7 copy.17
  7.2 0.6 pad_dynamic-slice_fusion.land_ref
  7.9 1.5 fusion.6
  9.3 80.1 %advect.1 = (f32[8,144,1024]{2,1,0:T(8,128)}, s16[8,144,1024]{2,1,0:T(8,128)(2,1)}, bf16[8,144,1152]{2,1,0:T(8,128)(2,1)}, bf16[8,144,1152]{2,1,0:T(8,128)(2,1)}...) custom-call(f32[2304,512]{1,0:T(8,128)} %bitcast.37, bf16[4,144,512]{2,1,0:T(8,128)(2,1)} %bitcast.39, ...), custom_call_target="tpu_custom_call" | custom-call | tf_op jit(solution)/shard_map/advect/pallas_call | solution.py:304
  89.4 0.0 copy-start.3
  89.4 0.0 copy-start.8
  89.4 2.7 %convert_multiply_fusion = f32[8,144,1024]{2,1,0:T(8,128)S(1)} fusion(s16[8,144,1024]{2,1,0:T(8,128)(2,1)} %get-tuple-element.15), kind=kLoop, calls=%fused_computation.5 | loop fusion | flops 2359296 | bytes 7077888 | tf_op jit(solution)/shard_map/mul | solution.py:494
  92.1 0.0 copy-done.3
  92.1 0.5 copy-done.8
  92.6 0.0 copy-start.7
  92.6 3.4 %fusion.2 = f32[1152,1024,1]{1,0,2:T(8,128)S(1)} fusion(bf16[8,144,1152]{2,1,0:T(8,128)(2,1)S(1)} %copy-done.8, s16[8,144,1024]{2,1,0:T(8,128)(2,1)S(1)} %copy-done.3), kind=kOutput, calls=%fused_computation.7 | convolution fusion | flops 2721447936 | bytes 9732096 | tf_op jit(solution)/shard_map/dot_general | solution.py:452
  95.9 0.0 copy-done.7
  95.9 0.0 copy-start.6
  96.0 3.7 %fusion = bf16[1152,1024]{1,0:T(8,128)(2,1)S(1)} fusion(f32[1152,1024,1]{1,0,2:T(8,128)S(1)} %fusion.2, bf16[8,144,1152]{2,1,0:T(8,128)(2,1)S(1)} %copy-done.7, s16[8,144,1024]{2,1,0:T(8,128)(2,1)S(1)} %copy-done.3), kind=kOutput, calls=%fused_computation.3 | convolution fusion | flops 2723807232 | bytes 12091392 | tf_op jit(solution)/shard_map/dot_general | solution.py:452
  99.6 0.0 copy-done.6
  99.6 0.0 copy-start.2
  99.6 3.3 %fusion.16 = f32[1152,1024]{1,0:T(8,128)S(1)} fusion(bf16[1152,1152]{1,0:T(8,128)(2,1)S(1)} %bitcast.47, bf16[1152,1024]{1,0:T(8,128)(2,1)S(1)} %fusion), kind=kOutput, calls=%fused_computation.31 | convolution fusion | flops 2717908992 | bytes 9732096 | tf_op jit(solution)/shard_map/dot_general | solution.py:452
  103.0 0.0 copy-done.2
  103.0 6.5 %bitcast_add_fusion = (f32[1152,1024]{1,0:T(8,128)}, bf16[1152,1024]{1,0:T(8,128)(2,1)}) fusion(f32[8,144,1024]{2,1,0:T(8,128)S(1)} %convert_multiply_fusion, f32[1152,1024]{1,0:T(8,128)S(1)} %fusion.16, f32[1152,1024]{1,0:T(8,128)S(1)} %bitcast.35, bf16[1152,1152]{1,0:T(8,128)(2,1)S(1)} %bitcast.36, bf16[1152,1024]{1,0:T(8,128)(2,1)S(1)} %fusion), kind=kOutput, calls=%fused_computation.1 | convolution fusion | flops 2723807232 | bytes 26247168 | tf_op jit(solution)/shard_map/dot_general | solution.py:452
  109.5 3.6 %all-to-all-start = ((bf16[8,144,1024]{2,1,0:T(8,128)(2,1)}), bf16[8,144,1024]{2,1,0:T(8,128)(2,1)S(1)}, u32[]{:S(2)}, u32[]{:S(2)}) async-start(bf16[8,144,1024]{2,1,0:T(8,128)(2,1)} %bitcast.9), calls=%async_computation | async-start | bytes 4718592 | tf_op jit(solution)/shard_map/all_to_all | solution.py:501
  113.8 0.0 copy-done
  113.8 6.1 %fusion.4.prof_ref = bf16[64,1024]{1,0:T(8,128)(2,1)} fusion(f32[1152,1024]{1,0:T(8,128)} %get-tuple-element.18, f32[1152,64]{0,1:T(8,128)S(1)} %copy-done), kind=kOutput, calls=%fused_computation.10 | convolution fusion | flops 906035200 | bytes 5144576 | tf_op jit(solution)/shard_map/dot_general | solution.py:498
  119.8 36.2 %ocean.1 = f32[64,2048]{1,0:T(8,128)} custom-call(bf16[64,1024]{1,0:T(8,128)(2,1)} %fusion.4.prof_ref, s32[1,2048]{1,0:T(1,128)} %bitcast.46, s32[2,2048]{1,0:T(2,128)} %bitcast.45, s32[1,1]{1,0:T(1,128)S(6)} %copy.21.count_ref, f32[64,2048]{1,0:T(8,128)} %bitcast.42, f32[64,2048]{1,0:T(8,128)} %bitcast.43), custom_call_target="tpu_custom_call" | custom-call | tf_op jit(solution)/shard_map/ocean/pallas_call | solution.py:436
  156.0 0.0 all-to-all-done.delta_ref
  156.0 0.0 copy-start.1
  156.0 1.4 copy-done.1
  157.5 0.0 copy-start.4
  157.5 10.3 %finish.1 = f32[2304,512]{1,0:T(8,128)} custom-call(f32[8,144,1024]{2,1,0:T(8,128)} %get-tuple-element.12.band_ref, bf16[8,144,1024]{2,1,0:T(8,128)(2,1)} %copy-done.1, bf16[512,512]{1,0:T(8,128)(2,1)} %get-tuple-element.22.ones_ref), custom_call_target="tpu_custom_call" | custom-call | tf_op jit(solution)/shard_map/finish/pallas_call | solution.py:358
  167.8 0.0 copy-done.4
  167.8 0.8 copy.22
  (3 shorter events, 0.0 us)
Async XLA Ops:
  0.6 113.2 %copy-start = (f32[1152,64]{0,1:T(8,128)S(1)}, f32[1152,64]{0,1:T(8,128)}, u32[]{:S(2)}) copy-start(f32[1152,64]{0,1:T(8,128)} %param.20) | copy-start | bytes 884740
  0.6 5.9 %copy-start.5 = (f32[2,144]{1,0:T(2,128)S(1)}, f32[2,144]{1,0:T(2,128)}, u32[]{:S(2)}) copy-start(f32[2,144]{1,0:T(2,128)} %param.15) | copy-start | bytes 3460
  89.4 2.7 %copy-start.3 = (s16[8,144,1024]{2,1,0:T(8,128)(2,1)S(1)}, s16[8,144,1024]{2,1,0:T(8,128)(2,1)}, u32[]{:S(2)}) copy-start(s16[8,144,1024]{2,1,0:T(8,128)(2,1)} %get-tuple-element.15) | copy-start | bytes 7077892
  89.4 3.2 %copy-start.8 = (bf16[8,144,1152]{2,1,0:T(8,128)(2,1)S(1)}, bf16[8,144,1152]{2,1,0:T(8,128)(2,1)}, u32[]{:S(2)}) copy-start(bf16[8,144,1152]{2,1,0:T(8,128)(2,1)} %get-tuple-element.14) | copy-start | bytes 7962628
  92.6 3.4 %copy-start.7 = (bf16[8,144,1152]{2,1,0:T(8,128)(2,1)S(1)}, bf16[8,144,1152]{2,1,0:T(8,128)(2,1)}, u32[]{:S(2)}) copy-start(bf16[8,144,1152]{2,1,0:T(8,128)(2,1)} %get-tuple-element.16) | copy-start | bytes 7962628
  95.9 3.7 %copy-start.6 = (bf16[8,144,1152]{2,1,0:T(8,128)(2,1)S(1)}, bf16[8,144,1152]{2,1,0:T(8,128)(2,1)}, u32[]{:S(2)}) copy-start(bf16[8,144,1152]{2,1,0:T(8,128)(2,1)} %get-tuple-element.13) | copy-start | bytes 7962628
  99.6 3.4 %copy-start.2 = (bf16[8,144,1152]{2,1,0:T(8,128)(2,1)S(1)}, bf16[8,144,1152]{2,1,0:T(8,128)(2,1)}, u32[]{:S(2)}) copy-start(bf16[8,144,1152]{2,1,0:T(8,128)(2,1)} %get-tuple-element.17) | copy-start | bytes 7962628
  109.5 46.5 %all-to-all-start = ((bf16[8,144,1024]{2,1,0:T(8,128)(2,1)}), bf16[8,144,1024]{2,1,0:T(8,128)(2,1)S(1)}, u32[]{:S(2)}, u32[]{:S(2)}) async-start(bf16[8,144,1024]{2,1,0:T(8,128)(2,1)} %bitcast.9), calls=%async_computation | async-start | bytes 4718592 | tf_op jit(solution)/shard_map/all_to_all | solution.py:501
  156.0 1.5 copy-start.1
  157.5 10.3 %copy-start.4 = (f32[64,2048]{1,0:T(8,128)S(1)}, f32[64,2048]{1,0:T(8,128)}, u32[]{:S(2)}) copy-start(f32[64,2048]{1,0:T(8,128)} %ocean.1) | copy-start | bytes 1572868

commit v4 on v3

--- a/solution.py
+++ b/solution.py
@@ -64,12 +64,12 @@
 
 
 def advect_kernel(
-    rows, dests, bands, x_ref, top_ref, end_ref, land_ref, cour_ref, ones_ref, wa, wb, wc, wd,
-    band_ref, pts_ref, ga, gb, gc, gd,
-    mask_ref, x_s, swept_s, a_s, b_s, u_s, up_s, dn_s, send_s, own_s,
-    halo_send, halo_recv, w_send, w_recv, p_send, p_recv, own_sem,
+    rows, dests, bands, x_ref, land_ref, cour_ref, wa, wb, wc, wd,
+    band_out, pts_ref, ga, gb, gc, gd,
+    mask_ref, ones_ref, x_all, band_ref, x_s, swept_s, a_s, b_s, u_s, top_s, end_s, up_s, dn_s, send_s, own_s,
+    halo_send, halo_recv, w_send, w_recv, p_send, p_recv, own_sem, band_sem, x_sem,
 ):
-    lon = ones_ref.shape[0]
+    lon = x_ref.shape[1]
     chunk = rows * lon // dests
     ways = lon // LANES
     margin = 2 * ADV
@@ -80,6 +80,8 @@
     bits = dests.bit_length() - 1
     shards, gathered = (wa, wb, wc, wd), (ga, gb, gc, gd)
 
+    x_copy = pltpu.make_async_copy(x_ref, x_all, x_sem)
+    x_copy.start()
     barrier = pltpu.get_barrier_semaphore()
     for k in range(1, dests):
         pl.semaphore_signal(barrier, inc=1, device_id={"comp": (me + k) % dests}, device_id_type=MESH)
@@ -95,25 +97,22 @@
     beside = (lat + bands - 1) // bands + (2 * (bands - 1) - lat) // bands
     pl.semaphore_wait(barrier, dests - 1 + beside)
 
-    def up_copy():
+    def block_at(i):
+        return pl.ds(pl.multiple_of(i * CB, CB), CB)
+
+    def up_copy(i):
         return pltpu.make_async_remote_copy(
-            src_ref=end_ref, dst_ref=up_s, send_sem=halo_send.at[0], recv_sem=halo_recv.at[0],
+            src_ref=end_s.at[:, block_at(i)], dst_ref=up_s.at[:, block_at(i)],
+            send_sem=halo_send.at[0, i], recv_sem=halo_recv.at[0, i],
             device_id={"lat": lat + 1}, device_id_type=MESH,
         )
 
-    def dn_copy():
+    def dn_copy(i):
         return pltpu.make_async_remote_copy(
-            src_ref=top_ref, dst_ref=dn_s, send_sem=halo_send.at[1], recv_sem=halo_recv.at[1],
+            src_ref=top_s.at[:, block_at(i)], dst_ref=dn_s.at[:, block_at(i)],
+            send_sem=halo_send.at[1, i], recv_sem=halo_recv.at[1, i],
             device_id={"lat": lat - 1}, device_id_type=MESH,
         )
-
-    @pl.when(lat + 1 < bands)
-    def _():
-        up_copy().start()
-
-    @pl.when(lat > 0)
-    def _():
-        dn_copy().start()
 
     orders = [[*range(1, bits), 0], [*range(bits - 1, 0, -1), 0]]
 
@@ -160,22 +159,43 @@
     def _():
         dn_s[...] = jnp.zeros_like(dn_s)
 
-    mask_ref[...] = jnp.dot(land_ref[...].astype(jnp.bfloat16), ones_ref[...], preferred_element_type=jnp.float32)
+    ones_ref[...] = spreader(lon)
+    height = land_ref.shape[0]
+    at_row = lax.broadcasted_iota(jnp.int32, (total, height), 0) + (lat * rows - margin)
+    rows_of = (lax.broadcasted_iota(jnp.int32, (total, height), 1) == at_row).astype(jnp.bfloat16)
+    land = land_ref[...].astype(jnp.float32).astype(jnp.bfloat16)
+    land = jnp.dot(rows_of, land, preferred_element_type=jnp.float32).astype(jnp.bfloat16)
+    mask_ref[...] = jnp.dot(land, ones_ref[...], preferred_element_type=jnp.float32)
+    x_copy.wait()
 
     @pl.loop(0, blocks)
     def _(i):
         size = CB * rows
-        whole = moved(x_ref[pl.ds(pl.multiple_of(i * size, size), size), :], ones_ref[...])
+        whole = moved(x_all[pl.ds(pl.multiple_of(i * size, size), size), :], ones_ref[...])
         for v in range(ways):
             x_s[v] = whole[:, v * LANES : (v + 1) * LANES]
-        for half in range(CB // 8):
-            base = pl.multiple_of(i * CB + half * 8, 8)
-            speed = speeds(cour_ref[pl.ds(base, 8), 0:1], lon)
-            for r in range(rows):
-                sea = mask_ref[margin + r : margin + r + 1, :]
-                first = half * (8 * rows) + r
+        halves = [pl.multiple_of(i * CB + h, 8) for h in range(0, CB, 8)]
+        paces = [speeds(cour_ref[pl.ds(base, 8), 0:1], lon) for base in halves]
+        for r in range(rows):
+            sea = mask_ref[margin + r : margin + r + 1, :]
+            lines = []
+            for h, base in enumerate(halves):
+                first = h * (8 * rows) + r
                 e = jnp.concatenate([x_s[v, pl.ds(first, 8, stride=rows), :] for v in range(ways)], axis=1)
-                swept_s[r, pl.ds(base, 8), :] = lon_row(e * sea, sea, speed)
+                lines.append(e)
+                swept_s[r, pl.ds(base, 8), :] = lon_row(e * sea, sea, paces[h])
+            if r < margin:
+                top_s[r, block_at(i), :] = jnp.concatenate(lines, axis=0).astype(jnp.bfloat16)
+            if r >= rows - margin:
+                end_s[r - (rows - margin), block_at(i), :] = jnp.concatenate(lines, axis=0).astype(jnp.bfloat16)
+
+        @pl.when(lat + 1 < bands)
+        def _():
+            up_copy(i).start()
+
+        @pl.when(lat > 0)
+        def _():
+            dn_copy(i).start()
 
     stores = [pltpu.make_async_copy(own_s.at[m], gathered[m].at[me], own_sem.at[4 + m]) for m in range(4)]
     for m in range(4):
@@ -185,13 +205,8 @@
     if bits > 1:
         weight_phase(1)
 
-    @pl.when(lat > 0)
-    def _():
-        up_copy().wait_recv()
-
-    @pl.when(lat + 1 < bands)
-    def _():
-        dn_copy().wait_recv()
+    def band_copy(i):
+        return pltpu.make_async_copy(band_ref.at[:, block_at(i)], band_out.at[:, block_at(i)], band_sem.at[i])
 
     def point_copy(k, i):
         to = (me + k) % dests
@@ -208,9 +223,18 @@
     @pl.loop(0, blocks)
     def _(i):
         both = pl.ds(pl.multiple_of(i * CB, CB), CB)
+
+        @pl.when(lat > 0)
+        def _():
+            up_copy(i).wait_recv()
+
+        @pl.when(lat + 1 < bands)
+        def _():
+            dn_copy(i).wait_recv()
+
         for k in range(2 * margin):
             src = up_s if k < margin else dn_s
-            u_s[k] = jnp.dot(src[k % margin, both, :], ones_ref[...], preferred_element_type=jnp.float32)
+            u_s[k] = src[k % margin, both, :].astype(jnp.float32)
 
         @pl.loop(0, CB // 8)
         def _(half):
@@ -265,6 +289,7 @@
             send_s[d, both, :] = value.astype(jnp.int32).astype(jnp.int16)
         for k in range(1, dests):
             point_copy(k, i).start()
+        band_copy(i).start()
 
     own_points = pltpu.make_async_copy(send_s.at[me], pts_ref.at[me], own_sem.at[8])
     own_points.start()
@@ -277,21 +302,23 @@
             for copy in weight_copies(m, phase):
                 copy.wait_send()
 
-    @pl.when(lat + 1 < bands)
-    def _():
-        up_copy().wait_send()
-
-    @pl.when(lat > 0)
-    def _():
-        dn_copy().wait_send()
-
     @pl.loop(0, blocks)
     def _(i):
+        band_copy(i).wait()
+
+        @pl.when(lat + 1 < bands)
+        def _():
+            up_copy(i).wait_send()
+
+        @pl.when(lat > 0)
+        def _():
+            dn_copy(i).wait_send()
+
         for k in range(1, dests):
             point_copy(k, i).wait()
 
 
-def advect(spectrum, top, end, mask_rows, cour, weights, dests, bands):
+def advect(spectrum, mask, cour, weights, dests, bands):
     comps, rows, lon = spectrum.shape
     chunk = rows * lon // dests
     margin = 2 * ADV
@@ -303,8 +330,8 @@
     dma = pltpu.SemaphoreType.DMA
     return pl.pallas_call(
         functools.partial(advect_kernel, rows, dests, bands),
-        in_specs=[vmem] * 6 + [hbm] * 4,
-        out_specs=[vmem] + [hbm] * 5,
+        in_specs=[hbm, vmem, vmem] + [hbm] * 4,
+        out_specs=[hbm] * 6,
         out_shape=[
             jax.ShapeDtypeStruct((dests, comps, chunk), jnp.float32),
             jax.ShapeDtypeStruct((dests, comps, chunk), jnp.int16),
@@ -312,33 +339,42 @@
         + [jax.ShapeDtypeStruct((dests, *shard), w.dtype) for w in weights],
         scratch_shapes=[
             pltpu.VMEM((total, lon), jnp.float32),
+            pltpu.VMEM((lon, lon), jnp.bfloat16),
+            pltpu.VMEM((comps * rows, lon), jnp.float32),
+            pltpu.VMEM((dests, comps, chunk), jnp.float32),
             pltpu.VMEM((lon // LANES, CB * rows, LANES), jnp.float32),
             pltpu.VMEM((rows, comps, lon), jnp.float32),
             pltpu.VMEM((total, 8, lon), jnp.float32),
             pltpu.VMEM((total, 8, lon), jnp.float32),
             pltpu.VMEM((2 * margin, CB, lon), jnp.float32),
-            pltpu.VMEM((margin, comps, lon), jnp.bfloat16),
-            pltpu.VMEM((margin, comps, lon), jnp.bfloat16),
+            *[pltpu.VMEM((margin, comps, lon), jnp.bfloat16)] * 4,
             pltpu.VMEM((dests, comps, chunk), jnp.int16),
             pltpu.VMEM((4, *shard), jnp.bfloat16),
-            dma((2,)),
-            dma((2,)),
+            dma((2, comps // CB)),
+            dma((2, comps // CB)),
             dma((4, copies)),
             dma((4, copies)),
             dma((copies, comps // CB)),
             dma((copies, comps // CB)),
             dma((9,)),
+            dma((comps // CB,)),
+            dma(()),
         ],
         compiler_params=pltpu.CompilerParams(
             collective_id=0, has_side_effects=True, vmem_limit_bytes=60 * 1024 * 1024
         ),
         name="advect",
-    )(spectrum.reshape(comps * rows, lon), top, end, mask_rows, cour, spreader(lon), *weights)
-
-
-def finish_kernel(rows, band_ref, delta_ref, ones_ref, out_ref, f_s):
+    )(spectrum.reshape(comps * rows, lon), mask, cour, *weights)
+
+
+def finish_kernel(rows, band_ref, delta_ref, out_ref, ones_ref, f_s):
     dests, cb, chunk = band_ref.shape
     lon = out_ref.shape[1]
+
+    @pl.when(pl.program_id(0) == 0)
+    def _():
+        ones_ref[...] = spreader(lon, back=True)
+
     for r in range(rows):
         at = 0
         while at < lon:
@@ -358,16 +394,22 @@
     out = pl.pallas_call(
         functools.partial(finish_kernel, rows),
         grid=(pl.cdiv(comps, CB),),
-        in_specs=[blk, blk, pl.BlockSpec((lon, lon), lambda i: (0, 0))],
+        in_specs=[blk, blk],
         out_specs=pl.BlockSpec((CB * rows, lon), lambda i: (i, 0)),
         out_shape=jax.ShapeDtypeStruct((comps * rows, lon), jnp.float32),
-        scratch_shapes=[pltpu.VMEM((lon // LANES, CB * rows, LANES), jnp.float32)],
+        scratch_shapes=[
+            pltpu.VMEM((lon, lon), jnp.bfloat16),
+            pltpu.VMEM((lon // LANES, CB * rows, LANES), jnp.float32),
+        ],
         name="finish",
-    )(band, delta, spreader(lon, back=True))
+    )(band, delta)
     return out.reshape(comps, rows, lon)
 
 
-def ocean_kernel(lon, prof_ref, pts_ref, nbr_ref, count_ref, vort_ref, diff_ref, out_ref, g_s, p_s, s_s, send, recv):
+def ocean_kernel(
+    lon, prof_ref, pts_ref, nbr_ref, count_ref, vort_ref, diff_ref, delta_ref, out_ref, back_ref,
+    g_s, p_s, s_s, own_s, send, recv, far_send, far_recv, own_sem,
+):
     dests, layers, chunk = g_s.shape
     slots = pts_ref.shape[1]
     per = LOW // layers
@@ -388,8 +430,21 @@
         )
         for k in range(1, dests)
     ]
-    for copy in copies:
+    returns = [
+        pltpu.make_async_remote_copy(
+            src_ref=delta_ref.at[(me + k) % dests],
+            dst_ref=back_ref.at[me],
+            send_sem=far_send.at[k - 1],
+            recv_sem=far_recv.at[k - 1],
+            device_id={"comp": (me + k) % dests},
+            device_id_type=MESH,
+        )
+        for k in range(1, dests)
+    ]
+    for copy in copies + returns:
         copy.start()
+    load = pltpu.make_async_copy(delta_ref.at[me], own_s, own_sem.at[0])
+    load.start()
     g_s[me] = prof_ref[...]
     s_s[...] = jnp.zeros_like(s_s)
     row = lax.broadcasted_iota(jnp.int32, (LOW, LOW), 0)
@@ -405,6 +460,9 @@
             acc = acc + jnp.where(high == m * per, product, 0.0)
         return sum(acc[i * layers : (i + 1) * layers] for i in range(per))
 
+    load.wait()
+    store = pltpu.make_async_copy(own_s, back_ref.at[me], own_sem.at[1])
+    store.start()
     for copy in copies:
         copy.wait()
     for d in range(dests):
@@ -426,26 +484,36 @@
         lower = jnp.concatenate([s[1:], jnp.zeros_like(s[:1])], axis=0)
         live = jnp.where(lane + j * LOW < count_ref[...], 1.0, 0.0)
         out_ref[:, part] = live * (vort_ref[:, part] * gap + diff_ref[:, part] * (upper - 2.0 * s + lower))
-
-
-def ocean(profile, pts, nbr, count, vort, diff, dests, lon):
+    store.wait()
+    for copy in returns:
+        copy.wait()
+
+
+def ocean(profile, pts, nbr, count, vort, diff, delta, lon):
+    dests = delta.shape[0]
     layers, chunk = profile.shape
     slots = pts.shape[1]
     per = LOW // layers
     depth = -(-(slots // LOW) // per) * LOW
     return pl.pallas_call(
         functools.partial(ocean_kernel, lon),
-        out_shape=jax.ShapeDtypeStruct((layers, slots), jnp.float32),
+        in_specs=[pl.BlockSpec(memory_space=pltpu.VMEM)] * 6 + [pl.BlockSpec(memory_space=pl.ANY)],
+        out_specs=[pl.BlockSpec(memory_space=pltpu.VMEM), pl.BlockSpec(memory_space=pl.ANY)],
+        out_shape=[
+            jax.ShapeDtypeStruct((layers, slots), jnp.float32),
+            jax.ShapeDtypeStruct(delta.shape, delta.dtype),
+        ],
         scratch_shapes=[
             pltpu.VMEM((dests, layers, chunk), profile.dtype),
             pltpu.VMEM((dests * chunk // LOW * layers, LOW), jnp.bfloat16),
             pltpu.VMEM((depth, LOW), jnp.bfloat16),
-            pltpu.SemaphoreType.DMA((dests - 1,)),
-            pltpu.SemaphoreType.DMA((dests - 1,)),
+            pltpu.VMEM(delta.shape[1:], delta.dtype),
+            *[pltpu.SemaphoreType.DMA((dests - 1,))] * 4,
+            pltpu.SemaphoreType.DMA((2,)),
         ],
         compiler_params=pltpu.CompilerParams(collective_id=1, has_side_effects=True),
         name="ocean",
-    )(profile, pts, nbr, count, vort, diff)
+    )(profile, pts, nbr, count, vort, diff, delta)
 
 
 def contract(weights, operand):
@@ -470,23 +538,16 @@
     diffusivity,
 ):
     comps, rows, lon = spectrum.shape
-    margin = 2 * ADV
     bands, dests = lax.axis_size("lat"), lax.axis_size("comp")
-    band_index = lax.axis_index("lat")
-    sea = jnp.pad(mask.astype(jnp.float32), ((margin, margin), (0, 0)))
-    mask_rows = lax.dynamic_slice_in_dim(sea, band_index * rows, rows + 2 * margin, 0)
     padded = pl.cdiv(comps, CB) * CB
     spread = ((0, padded - comps), (0, 0), (0, 0))
-    top, end = lax.optimization_barrier((spectrum[:, :margin], spectrum[:, rows - margin :]))
-    top, end = (part.astype(jnp.bfloat16).transpose(1, 0, 2) for part in (top, end))
     weights = (proj_a, proj_b, proj_c, proj_d)
     cour = courant.T
     start = spectrum
     if padded != comps:
         start = jnp.pad(spectrum, spread)
         cour = jnp.pad(cour, spread[:2])
-        top, end = (jnp.pad(part, (spread[1], spread[0], spread[2])) for part in (top, end))
-    band, points, *weights = advect(start, top, end, mask_rows, cour, weights, dests, bands)
+    band, points, *weights = advect(start, mask, cour, weights, dests, bands)
     band, points = band[:, :comps], points[:, :comps]
     weights = [w.reshape(dests * comps, -1) for w in weights]
     chunk = points.shape[2]
@@ -498,11 +559,9 @@
     profile = lax.dot_general(
         stokes_kernel, own + delta, (((0,), (0,)), ((), ())), precision=lax.Precision.HIGHEST
     ).astype(jnp.bfloat16)
-    back = lax.all_to_all(
-        delta.astype(jnp.bfloat16).reshape(dests, comps, chunk), "comp", split_axis=0, concat_axis=0
-    )
-    force = ocean(
-        profile, tile_points[0], tile_nbr[0, 0], tile_counts, vorticity[0, 0], diffusivity[0, 0], dests, lon
+    force, back = ocean(
+        profile, tile_points[0], tile_nbr[0, 0], tile_counts, vorticity[0, 0], diffusivity[0, 0],
+        delta.astype(jnp.bfloat16).reshape(dests, comps, chunk), lon,
     )
     return finish(band, back, rows, lon), force[None, None]
 

time: 170 us -> 157 us (0.924)
  local copies, waits for them, and re-layouts: 8.93 us -> 3.16 us
  other arithmetic: 5.11 us -> 0.86 us
  starting transfers between devices: 3.64 us -> 0 us
  Pallas kernels: 127 us -> 129 us
    pallas_call x1, Pallas kernels: 36.2 us -> 41.9 us  [ocean(): pl.pallas_call(functools.partial(ocean_kernel, lon), in_specs=[pl.BlockSp...]
    all_to_all x1 -> x0, starting transfers between devices: 3.64 us -> none  [on_device(): lax.all_to_all(delta.astype(jnp.bfloat16).reshape(dests, comps, chunk), '...]
    pallas_call x1, Pallas kernels: 80.1 us -> 76.4 us  [advect(): pl.pallas_call(functools.partial(advect_kernel, rows, dests, bands), in_s...]
    slice x1 -> x0, local copies, waits for them, and re-layouts: 2.97 us -> none  [on_device(): spectrum[:, rows - margin:]]
    convert_element_type x2 -> x0, other arithmetic: 2.42 us -> none  [the longest x1 1.47 us: spreader(): return (x == at % LANES * ways + at // LANES).astype(jnp.bfloat16)]
    dot_general x1, matrix products: 6.06 us -> 3.79 us  [on_device(): lax.dot_general(stokes_kernel, own + delta, (((0,), (0,)), ((), ())), pre...]
    optimization_barrier x2 -> x0, local copies, waits for them, and re-layouts: 1.88 us -> none  [on_device(): lax.optimization_barrier((spectrum[:, :margin], spectrum[:, rows - margin...]
    mul x1, other arithmetic: 2.67 us -> 0.86 us  [on_device(): own = points.astype(jnp.float32) * (1.0 / STEPS)]
  transfers between devices with their start and end apart: 1 -> 0, of which waited for: 0 -> 0; matrix products, arithmetic and copies ran while one was open for 4% -> 0% of each run, Pallas kernels for 21% -> 0%
where the time goes in v4:
time: 157 us; the launch traced here: 156 us
  Pallas kernels  129 us (82%)
  matrix products  22.2 us (14%)
  local copies, waits for them, and re-layouts  3.16 us (2%)
    pallas_call x1, Pallas kernels, advect(): pl.pallas_call(functools.partial(advect_kernel, rows, dests, bands), in_s...  76.4 us
    pallas_call x1, Pallas kernels, ocean(): pl.pallas_call(functools.partial(ocean_kernel, lon), in_specs=[pl.BlockSp...  41.9 us
    dot_general x4, matrix products, contract(): lax.dot_general(weights, operand, (((0,), (0,)), ((), ())), preferred_ele...  18.4 us
    pallas_call x1, Pallas kernels, finish(): pl.pallas_call(functools.partial(finish_kernel, rows), grid=(pl.cdiv(comp...  10.3 us
    dot_general x1, matrix products, on_device(): lax.dot_general(stokes_kernel, own + delta, (((0,), (0,)), ((), ())), pre...  3.79 us
    unnamed x14, local copies, waits for them, and re-layouts  3.16 us

profile of v4, /device:TPU:0, one launch (start us, length us, event | category | flops | bytes accessed | tf_op | source)
XLA Modules:
  0.0 156.2 jit_solution(16890298133850938226)
XLA Ops:
  0.6 0.0 copy-start
  0.6 1.5 copy.15
  2.1 76.4 %advect.1 = (f32[8,144,1024]{2,1,0:T(8,128)}, s16[8,144,1024]{2,1,0:T(8,128)(2,1)}, bf16[8,144,1152]{2,1,0:T(8,128)(2,1)}, bf16[8,144,1152]{2,1,0:T(8,128)(2,1)}...) custom-call(f32[2304,512]{1,0:T(8,128)} %bitcast.32, s32[64,512]{1,0:T(8,128)} %land_ref.1, ...), custom_call_target="tpu_custom_call" | custom-call | tf_op jit(solution)/shard_map/advect/pallas_call | solution.py:331
  78.5 0.0 copy-start.2
  78.6 0.0 copy-start.5
  78.6 5.9 %fusion.2 = f32[1152,1024,1]{1,0,2:T(8,128)S(1)} fusion(bf16[8,144,1152]{2,1,0:T(8,128)(2,1)} %get-tuple-element.13, s16[8,144,1024]{2,1,0:T(8,128)(2,1)} %get-tuple-element.11), kind=kOutput, calls=%fused_computation.7 | convolution fusion | flops 2721447936 | bytes 9732096 | tf_op jit(solution)/shard_map/dot_general | solution.py:520
  84.5 0.0 copy-done.2
  84.5 0.0 copy-done.5
  84.5 0.0 copy-start.4
  84.6 3.8 %fusion = bf16[1152,1024]{1,0:T(8,128)(2,1)S(1)} fusion(f32[1152,1024,1]{1,0,2:T(8,128)S(1)} %fusion.2, bf16[8,144,1152]{2,1,0:T(8,128)(2,1)S(1)} %copy-done.5, s16[8,144,1024]{2,1,0:T(8,128)(2,1)S(1)} %copy-done.2), kind=kOutput, calls=%fused_computation.2 | convolution fusion | flops 2723807232 | bytes 12091392 | tf_op jit(solution)/shard_map/dot_general | solution.py:520
  88.4 0.0 copy-done.4
  88.4 3.3 %fusion.8 = f32[1152,1024]{1,0:T(8,128)S(1)} fusion(bf16[1152,1152]{1,0:T(8,128)(2,1)S(1)} %bitcast.40, bf16[1152,1024]{1,0:T(8,128)(2,1)S(1)} %fusion), kind=kOutput, calls=%fused_computation.14 | convolution fusion | flops 2717908992 | bytes 9732096 | tf_op jit(solution)/shard_map/dot_general | solution.py:520
  91.7 0.0 copy-start.1
  91.7 0.9 convert_multiply_fusion
  92.6 0.9 copy-done.1
  93.5 5.4 %fusion.7 = (bf16[1152,1024]{1,0:T(8,128)(2,1)}, f32[1152,1024]{1,0:T(8,128)S(1)}) fusion(f32[8,144,1024]{2,1,0:T(8,128)S(1)} %convert_multiply_fusion, f32[1152,1024]{1,0:T(8,128)S(1)} %fusion.8, f32[1152,1024]{1,0:T(8,128)S(1)} %bitcast.29, bf16[1152,1152]{1,0:T(8,128)(2,1)S(1)} %bitcast.31, bf16[1152,1024]{1,0:T(8,128)(2,1)S(1)} %fusion), kind=kOutput, calls=%fused_computation.13 | convolution fusion | flops 2723807232 | bytes 26247168 | tf_op jit(solution)/shard_map/dot_general | solution.py:520
  98.8 0.0 copy-done
  98.8 3.8 %fusion.4.prof_ref = bf16[64,1024]{1,0:T(8,128)(2,1)} fusion(f32[1152,1024]{1,0:T(8,128)S(1)} %get-tuple-element.19, f32[1152,64]{0,1:T(8,128)S(1)} %copy-done), kind=kOutput, calls=%fused_computation.10 | convolution fusion | flops 906035200 | bytes 5144576 | tf_op jit(solution)/shard_map/dot_general | solution.py:559
  103.3 41.9 %ocean.1 = (f32[64,2048]{1,0:T(8,128)}, bf16[8,144,1024]{2,1,0:T(8,128)(2,1)}) custom-call(bf16[64,1024]{1,0:T(8,128)(2,1)} %fusion.4.prof_ref, s32[1,2048]{1,0:T(1,128)} %bitcast.39, s32[2,2048]{1,0:T(2,128)} %bitcast.38, s32[1,1]{1,0:T(1,128)S(6)} %copy.17.count_ref, f32[64,2048]{1,0:T(8,128)} %bitcast.35, f32[64,2048]{1,0:T(8,128)} %bitcast.36, ...), custom_call_target="tpu_custom_call" | custom-call | tf_op jit(solution)/shard_map/ocean/pallas_call | solution.py:498
  145.1 0.0 copy-start.3
  145.1 10.3 %finish.1 = f32[2304,512]{1,0:T(8,128)} custom-call(f32[8,144,1024]{2,1,0:T(8,128)} %get-tuple-element.10.band_ref, bf16[8,144,1024]{2,1,0:T(8,128)(2,1)} %get-tuple-element.16.delta_ref), custom_call_target="tpu_custom_call" | custom-call | tf_op jit(solution)/shard_map/finish/pallas_call | solution.py:394
  155.4 0.0 copy-done.3
  155.4 0.8 copy.18
Async XLA Ops:
  0.6 98.2 %copy-start = (f32[1152,64]{0,1:T(8,128)S(1)}, f32[1152,64]{0,1:T(8,128)}, u32[]{:S(2)}) copy-start(f32[1152,64]{0,1:T(8,128)} %param.20) | copy-start | bytes 884740
  78.5 6.0 %copy-start.2 = (s16[8,144,1024]{2,1,0:T(8,128)(2,1)S(1)}, s16[8,144,1024]{2,1,0:T(8,128)(2,1)}, u32[]{:S(2)}) copy-start(s16[8,144,1024]{2,1,0:T(8,128)(2,1)} %get-tuple-element.11) | copy-start | bytes 7077892
  78.6 6.0 %copy-start.5 = (bf16[8,144,1152]{2,1,0:T(8,128)(2,1)S(1)}, bf16[8,144,1152]{2,1,0:T(8,128)(2,1)}, u32[]{:S(2)}) copy-start(bf16[8,144,1152]{2,1,0:T(8,128)(2,1)} %get-tuple-element.14) | copy-start | bytes 7962628
  84.5 3.8 %copy-start.4 = (bf16[8,144,1152]{2,1,0:T(8,128)(2,1)S(1)}, bf16[8,144,1152]{2,1,0:T(8,128)(2,1)}, u32[]{:S(2)}) copy-start(bf16[8,144,1152]{2,1,0:T(8,128)(2,1)} %get-tuple-element.12) | copy-start | bytes 7962628
  91.7 1.8 %copy-start.1 = (bf16[8,144,1152]{2,1,0:T(8,128)(2,1)S(1)}, bf16[8,144,1152]{2,1,0:T(8,128)(2,1)}, u32[]{:S(2)}) copy-start(bf16[8,144,1152]{2,1,0:T(8,128)(2,1)} %get-tuple-element.15) | copy-start | bytes 7962628
  145.1 10.3 %copy-start.3 = (f32[64,2048]{1,0:T(8,128)S(1)}, f32[64,2048]{1,0:T(8,128)}, u32[]{:S(2)}) copy-start(f32[64,2048]{1,0:T(8,128)} %get-tuple-element.17) | copy-start | bytes 1572868

commit v5 on v4

--- a/solution.py
+++ b/solution.py
@@ -367,35 +367,38 @@
     )(spectrum.reshape(comps * rows, lon), mask, cour, *weights)
 
 
-def finish_kernel(rows, band_ref, delta_ref, out_ref, ones_ref, f_s):
-    dests, cb, chunk = band_ref.shape
-    lon = out_ref.shape[1]
-
-    @pl.when(pl.program_id(0) == 0)
-    def _():
-        ones_ref[...] = spreader(lon, back=True)
-
+def lay_rows(rows, lon, part, f_s):
+    dests, cb, chunk = part.shape
     for r in range(rows):
         at = 0
         while at < lon:
             d, lane = divmod(r * lon + at, chunk)
             n = min(chunk - lane, lon - at)
-            v = band_ref[d, :, lane : lane + n] + delta_ref[d, :, lane : lane + n].astype(jnp.float32)
+            v = part[d, :, lane : lane + n].astype(jnp.float32)
             for j in range(n // LANES):
                 f_s[at // LANES + j, pl.ds(r, cb, stride=rows), :] = v[:, j * LANES : (j + 1) * LANES]
             at += n
-    whole = jnp.concatenate([f_s[v] for v in range(lon // LANES)], axis=1)
-    out_ref[...] = moved(whole, ones_ref[...])
-
-
-def finish(band, delta, rows, lon):
-    dests, comps, chunk = band.shape
-    blk = pl.BlockSpec((dests, CB, chunk), lambda i: (0, i, 0))
+    return jnp.concatenate([f_s[v] for v in range(lon // LANES)], axis=1)
+
+
+def finish_kernel(rows, band_ref, delta_ref, out_ref, ones_ref, f_s):
+    @pl.when(pl.program_id(0) == 0)
+    def _():
+        ones_ref[...] = spreader(out_ref.shape[1], back=True)
+
+    whole = lay_rows(rows, out_ref.shape[1], delta_ref, f_s).astype(jnp.bfloat16)
+    out_ref[...] = band_ref[...] + jnp.dot(whole, ones_ref[...], preferred_element_type=jnp.float32)
+
+
+def finish(band, delta, rows):
+    dests, comps, chunk = delta.shape
+    lon = band.shape[1]
+    line = pl.BlockSpec((CB * rows, lon), lambda i: (i, 0))
     out = pl.pallas_call(
         functools.partial(finish_kernel, rows),
         grid=(pl.cdiv(comps, CB),),
-        in_specs=[blk, blk],
-        out_specs=pl.BlockSpec((CB * rows, lon), lambda i: (i, 0)),
+        in_specs=[line, pl.BlockSpec((dests, CB, chunk), lambda i: (0, i, 0))],
+        out_specs=line,
         out_shape=jax.ShapeDtypeStruct((comps * rows, lon), jnp.float32),
         scratch_shapes=[
             pltpu.VMEM((lon, lon), jnp.bfloat16),
@@ -407,14 +410,18 @@
 
 
 def ocean_kernel(
-    lon, prof_ref, pts_ref, nbr_ref, count_ref, vort_ref, diff_ref, delta_ref, out_ref, back_ref,
-    g_s, p_s, s_s, own_s, send, recv, far_send, far_recv, own_sem,
+    lon, prof_ref, pts_ref, nbr_ref, count_ref, vort_ref, diff_ref, delta_ref, band_ref, out_ref, back_ref, line_ref,
+    g_s, p_s, s_s, own_s, band_s, line_s, f_s, ones_s, send, recv, far_send, far_recv, own_sem, line_sem,
 ):
     dests, layers, chunk = g_s.shape
     slots = pts_ref.shape[1]
     per = LOW // layers
     ways = lon // LANES
+    rows = dests * chunk // lon
+    blocks = band_s.shape[1] // CB
     me = lax.axis_index("comp")
+    band_load = pltpu.make_async_copy(band_ref, band_s, own_sem.at[2])
+    band_load.start()
     barrier = pltpu.get_barrier_semaphore()
     for k in range(1, dests):
         pl.semaphore_signal(barrier, inc=1, device_id={"comp": (me + k) % dests}, device_id_type=MESH)
@@ -484,36 +491,62 @@
         lower = jnp.concatenate([s[1:], jnp.zeros_like(s[:1])], axis=0)
         live = jnp.where(lane + j * LOW < count_ref[...], 1.0, 0.0)
         out_ref[:, part] = live * (vort_ref[:, part] * gap + diff_ref[:, part] * (upper - 2.0 * s + lower))
+    band_load.wait()
+    ones_s[...] = spreader(lon, back=True)
+
+    def line_copy(i):
+        at = pl.ds(pl.multiple_of(i * (CB * rows), CB * rows), CB * rows)
+        return pltpu.make_async_copy(line_s.at[at], line_ref.at[at], line_sem.at[i])
+
+    @pl.loop(0, blocks)
+    def _(i):
+        part = band_s.at[:, pl.ds(pl.multiple_of(i * CB, CB), CB)]
+        at = pl.ds(pl.multiple_of(i * (CB * rows), CB * rows), CB * rows)
+        line_s[at, :] = moved(lay_rows(rows, lon, part, f_s), ones_s[...])
+        line_copy(i).start()
+
     store.wait()
     for copy in returns:
         copy.wait()
 
-
-def ocean(profile, pts, nbr, count, vort, diff, delta, lon):
+    @pl.loop(0, blocks)
+    def _(i):
+        line_copy(i).wait()
+
+
+def ocean(profile, pts, nbr, count, vort, diff, delta, band, lon):
     dests = delta.shape[0]
+    comps = band.shape[1]
+    rows = dests * band.shape[2] // lon
     layers, chunk = profile.shape
     slots = pts.shape[1]
     per = LOW // layers
     depth = -(-(slots // LOW) // per) * LOW
     return pl.pallas_call(
         functools.partial(ocean_kernel, lon),
-        in_specs=[pl.BlockSpec(memory_space=pltpu.VMEM)] * 6 + [pl.BlockSpec(memory_space=pl.ANY)],
-        out_specs=[pl.BlockSpec(memory_space=pltpu.VMEM), pl.BlockSpec(memory_space=pl.ANY)],
+        in_specs=[pl.BlockSpec(memory_space=pltpu.VMEM)] * 6 + [pl.BlockSpec(memory_space=pl.ANY)] * 2,
+        out_specs=[pl.BlockSpec(memory_space=pltpu.VMEM)] + [pl.BlockSpec(memory_space=pl.ANY)] * 2,
         out_shape=[
             jax.ShapeDtypeStruct((layers, slots), jnp.float32),
             jax.ShapeDtypeStruct(delta.shape, delta.dtype),
+            jax.ShapeDtypeStruct((comps * rows, lon), jnp.float32),
         ],
         scratch_shapes=[
             pltpu.VMEM((dests, layers, chunk), profile.dtype),
             pltpu.VMEM((dests * chunk // LOW * layers, LOW), jnp.bfloat16),
             pltpu.VMEM((depth, LOW), jnp.bfloat16),
             pltpu.VMEM(delta.shape[1:], delta.dtype),
+            pltpu.VMEM(band.shape, jnp.float32),
+            pltpu.VMEM((comps * rows, lon), jnp.float32),
+            pltpu.VMEM((lon // LANES, CB * rows, LANES), jnp.float32),
+            pltpu.VMEM((lon, lon), jnp.bfloat16),
             *[pltpu.SemaphoreType.DMA((dests - 1,))] * 4,
-            pltpu.SemaphoreType.DMA((2,)),
+            pltpu.SemaphoreType.DMA((3,)),
+            pltpu.SemaphoreType.DMA((comps // CB,)),
         ],
         compiler_params=pltpu.CompilerParams(collective_id=1, has_side_effects=True),
         name="ocean",
-    )(profile, pts, nbr, count, vort, diff, delta)
+    )(profile, pts, nbr, count, vort, diff, delta, band)
 
 
 def contract(weights, operand):
@@ -548,7 +581,7 @@
         start = jnp.pad(spectrum, spread)
         cour = jnp.pad(cour, spread[:2])
     band, points, *weights = advect(start, mask, cour, weights, dests, bands)
-    band, points = band[:, :comps], points[:, :comps]
+    points = points[:, :comps]
     weights = [w.reshape(dests * comps, -1) for w in weights]
     chunk = points.shape[2]
     points = points.reshape(dests * comps, chunk)
@@ -559,11 +592,11 @@
     profile = lax.dot_general(
         stokes_kernel, own + delta, (((0,), (0,)), ((), ())), precision=lax.Precision.HIGHEST
     ).astype(jnp.bfloat16)
-    force, back = ocean(
+    force, back, lines = ocean(
         profile, tile_points[0], tile_nbr[0, 0], tile_counts, vorticity[0, 0], diffusivity[0, 0],
-        delta.astype(jnp.bfloat16).reshape(dests, comps, chunk), lon,
+        delta.astype(jnp.bfloat16).reshape(dests, comps, chunk), band, lon,
     )
-    return finish(band, back, rows, lon), force[None, None]
+    return finish(lines, back, rows), force[None, None]
 
 
 def solution(mesh):

time: 157 us -> 157 us (level)
  no operation moved by 1% of the time
where the time goes in v5:
time: 157 us; the launch traced here: 156 us
  Pallas kernels  128 us (82%)
  matrix products  22.2 us (14%)
  local copies, waits for them, and re-layouts  3.16 us (2%)
    pallas_call x1, Pallas kernels, advect(): pl.pallas_call(functools.partial(advect_kernel, rows, dests, bands), in_s...  76.4 us
    pallas_call x1, Pallas kernels, ocean(): pl.pallas_call(functools.partial(ocean_kernel, lon), in_specs=[pl.BlockSp...  42 us
    dot_general x4, matrix products, contract(): lax.dot_general(weights, operand, (((0,), (0,)), ((), ())), preferred_ele...  18.4 us
    pallas_call x1, Pallas kernels, finish(): pl.pallas_call(functools.partial(finish_kernel, rows), grid=(pl.cdiv(comp...  9.66 us
    dot_general x1, matrix products, on_device(): lax.dot_general(stokes_kernel, own + delta, (((0,), (0,)), ((), ())), pre...  3.79 us
    unnamed x14, local copies, waits for them, and re-layouts  3.16 us

profile of v5, /device:TPU:0, one launch (start us, length us, event | category | flops | bytes accessed | tf_op | source)
XLA Modules:
  0.0 155.7 jit_solution(13748321646139029826)
XLA Ops:
  0.6 0.0 copy-start
  0.6 1.5 copy.15
  2.1 76.4 %advect.1 = (f32[8,144,1024]{2,1,0:T(8,128)}, s16[8,144,1024]{2,1,0:T(8,128)(2,1)}, bf16[8,144,1152]{2,1,0:T(8,128)(2,1)}, bf16[8,144,1152]{2,1,0:T(8,128)(2,1)}...) custom-call(f32[2304,512]{1,0:T(8,128)} %bitcast.32, s32[64,512]{1,0:T(8,128)} %land_ref.1, ...), custom_call_target="tpu_custom_call" | custom-call | tf_op jit(solution)/shard_map/advect/pallas_call | solution.py:331
  78.5 0.0 copy-start.2
  78.6 0.0 copy-start.5
  78.6 5.9 %fusion.2 = f32[1152,1024,1]{1,0,2:T(8,128)S(1)} fusion(bf16[8,144,1152]{2,1,0:T(8,128)(2,1)} %get-tuple-element.13, s16[8,144,1024]{2,1,0:T(8,128)(2,1)} %get-tuple-element.11), kind=kOutput, calls=%fused_computation.7 | convolution fusion | flops 2721447936 | bytes 9732096 | tf_op jit(solution)/shard_map/dot_general | solution.py:553
  84.5 0.0 copy-done.2
  84.5 0.0 copy-done.5
  84.5 0.0 copy-start.4
  84.6 3.8 %fusion = bf16[1152,1024]{1,0:T(8,128)(2,1)S(1)} fusion(f32[1152,1024,1]{1,0,2:T(8,128)S(1)} %fusion.2, bf16[8,144,1152]{2,1,0:T(8,128)(2,1)S(1)} %copy-done.5, s16[8,144,1024]{2,1,0:T(8,128)(2,1)S(1)} %copy-done.2), kind=kOutput, calls=%fused_computation.2 | convolution fusion | flops 2723807232 | bytes 12091392 | tf_op jit(solution)/shard_map/dot_general | solution.py:553
  88.4 0.0 copy-done.4
  88.4 3.3 %fusion.8 = f32[1152,1024]{1,0:T(8,128)S(1)} fusion(bf16[1152,1152]{1,0:T(8,128)(2,1)S(1)} %bitcast.40, bf16[1152,1024]{1,0:T(8,128)(2,1)S(1)} %fusion), kind=kOutput, calls=%fused_computation.14 | convolution fusion | flops 2717908992 | bytes 9732096 | tf_op jit(solution)/shard_map/dot_general | solution.py:553
  91.7 0.0 copy-start.1
  91.7 0.9 convert_multiply_fusion
  92.6 0.9 copy-done.1
  93.5 5.4 %fusion.7 = (bf16[1152,1024]{1,0:T(8,128)(2,1)}, f32[1152,1024]{1,0:T(8,128)S(1)}) fusion(f32[8,144,1024]{2,1,0:T(8,128)S(1)} %convert_multiply_fusion, f32[1152,1024]{1,0:T(8,128)S(1)} %fusion.8, f32[1152,1024]{1,0:T(8,128)S(1)} %bitcast.29, bf16[1152,1152]{1,0:T(8,128)(2,1)S(1)} %bitcast.31, bf16[1152,1024]{1,0:T(8,128)(2,1)S(1)} %fusion), kind=kOutput, calls=%fused_computation.13 | convolution fusion | flops 2723807232 | bytes 26247168 | tf_op jit(solution)/shard_map/dot_general | solution.py:553
  98.8 0.0 copy-done
  98.8 3.8 %fusion.4.prof_ref = bf16[64,1024]{1,0:T(8,128)(2,1)} fusion(f32[1152,1024]{1,0:T(8,128)S(1)} %get-tuple-element.21, f32[1152,64]{0,1:T(8,128)S(1)} %copy-done), kind=kOutput, calls=%fused_computation.10 | convolution fusion | flops 906035200 | bytes 5144576 | tf_op jit(solution)/shard_map/dot_general | solution.py:592
  103.3 42.0 %ocean.1 = (f32[64,2048]{1,0:T(8,128)}, bf16[8,144,1024]{2,1,0:T(8,128)(2,1)}, f32[2304,512]{1,0:T(8,128)}) custom-call(bf16[64,1024]{1,0:T(8,128)(2,1)} %fusion.4.prof_ref, s32[1,2048]{1,0:T(1,128)} %bitcast.39, s32[2,2048]{1,0:T(2,128)} %bitcast.38, s32[1,1]{1,0:T(1,128)S(6)} %copy.17.count_ref, f32[64,2048]{1,0:T(8,128)} %bitcast.34, ...), custom_call_target="tpu_custom_call" | custom-call | tf_op jit(solution)/shard_map/ocean/pallas_call | solution.py:525
  145.2 0.0 copy-start.3
  145.3 9.7 %finish.1 = f32[2304,512]{1,0:T(8,128)} custom-call(f32[2304,512]{1,0:T(8,128)} %get-tuple-element.17.band_ref, bf16[8,144,1024]{2,1,0:T(8,128)(2,1)} %get-tuple-element.18.delta_ref), custom_call_target="tpu_custom_call" | custom-call | tf_op jit(solution)/shard_map/finish/pallas_call | solution.py:397
  154.9 0.0 copy-done.3
  154.9 0.8 copy.18
Async XLA Ops:
  0.6 98.2 %copy-start = (f32[1152,64]{0,1:T(8,128)S(1)}, f32[1152,64]{0,1:T(8,128)}, u32[]{:S(2)}) copy-start(f32[1152,64]{0,1:T(8,128)} %param.20) | copy-start | bytes 884740
  78.5 6.0 %copy-start.2 = (s16[8,144,1024]{2,1,0:T(8,128)(2,1)S(1)}, s16[8,144,1024]{2,1,0:T(8,128)(2,1)}, u32[]{:S(2)}) copy-start(s16[8,144,1024]{2,1,0:T(8,128)(2,1)} %get-tuple-element.11) | copy-start | bytes 7077892
  78.6 6.0 %copy-start.5 = (bf16[8,144,1152]{2,1,0:T(8,128)(2,1)S(1)}, bf16[8,144,1152]{2,1,0:T(8,128)(2,1)}, u32[]{:S(2)}) copy-start(bf16[8,144,1152]{2,1,0:T(8,128)(2,1)} %get-tuple-element.14) | copy-start | bytes 7962628
  84.5 3.8 %copy-start.4 = (bf16[8,144,1152]{2,1,0:T(8,128)(2,1)S(1)}, bf16[8,144,1152]{2,1,0:T(8,128)(2,1)}, u32[]{:S(2)}) copy-start(bf16[8,144,1152]{2,1,0:T(8,128)(2,1)} %get-tuple-element.12) | copy-start | bytes 7962628
  91.7 1.8 %copy-start.1 = (bf16[8,144,1152]{2,1,0:T(8,128)(2,1)S(1)}, bf16[8,144,1152]{2,1,0:T(8,128)(2,1)}, u32[]{:S(2)}) copy-start(bf16[8,144,1152]{2,1,0:T(8,128)(2,1)} %get-tuple-element.15) | copy-start | bytes 7962628
  145.2 9.7 %copy-start.3 = (f32[64,2048]{1,0:T(8,128)S(1)}, f32[64,2048]{1,0:T(8,128)}, u32[]{:S(2)}) copy-start(f32[64,2048]{1,0:T(8,128)} %get-tuple-element.19) | copy-start | bytes 1572868
